TPU v7x, 32 devices: a whole 2x2x4 slice. The times are simulated.
32 devices in a mesh: grp: 2 (over y), seq: 4 (over z), sub: 2 (over x), rep: 2 (over core).
Axes of the slice: x: 2, y: 2, z: 4, core: 2. Of those that a mesh axis runs over, the one named last changes fastest.
Arguments:
- query_proj: bfloat16 [2048, 1536], P(('grp', 'seq'), ('sub', 'rep')), parts along dimension 0, may hold values from -5 to 5
- key_proj: bfloat16 [2048, 1536], P(('grp', 'seq'), ('sub', 'rep')), parts along dimension 0, may hold values from -5 to 5
- value_proj: bfloat16 [2048, 1536], P(('grp', 'seq'), ('sub', 'rep')), parts along dimension 0, may hold values from -8 to 8
- block_mask: int32 [24, 8, 8], P(('grp', 'sub', 'rep')), parts along dimension 0, may hold values from 0 to 1, as said below
- unit_plan: int32 [8, 4, 3], P(('grp', 'sub', 'rep')), parts along dimension 0, may hold values from 0 to 8, as said below
- out_weight: bfloat16 [1536, 3072], P(('sub', 'rep')), may hold values from -0.15625 to 0.15625
Outputs:
- attn_out: bfloat16 [2048, 3072], P(('grp', 'seq', 'sub', 'rep')), parts along dimension 0
- unit_logsum: float32 [8, 4, 1024], P(('grp', 'sub', 'rep'), 'seq'), parts along dimension 0
There are 2 independent parts, one for each index of `grp`. A program takes and returns all parts, laid end to end along the dimension named above; an argument that names none is the same for every part. Nothing has to cross between parts.
Inputs may be any that keep to these rules, and one draw needn't show every extreme that they name: block_mask[h, b, b] = 1 for every head and block; every row holds 1 to 4 ones, and every head has a row with exactly 4. unit_plan[g, d] = (h, b, n): the device of index d along seq in head group g owns head h of the group's 3 heads, query blocks b to b + n - 1. For every head the units of the group cover its 8 query blocks exactly once; every head has at least one unit; n is 1 to 8, and some unit of every group has exactly 8.
All inputs are finite; a program needn't handle non-finite values.
Results may differ from a plain program's by a relative error of at most 0.0075.
Values may be sent and summed in bfloat16 or wider, within the bound.
A program may use at most 128 MiB of HBM per device.

v0:
```python
import math

import jax
import jax.numpy as jnp
from jax import lax
from jax.sharding import PartitionSpec as P

DH = 128
BLK = 128


def by_owner(local_rows, owners):
    result = jnp.zeros(
        (owners.shape[0],) + local_rows.shape[:1] + local_rows.shape[2:], local_rows.dtype
    )
    for which_head in range(local_rows.shape[1]):
        matches = (owners == which_head).reshape((-1,) + (1,) * (local_rows.ndim - 1))
        result = jnp.where(matches, local_rows[:, which_head][None], result)
    return result


def key_lists_of(mask_rows, key_most):
    key_order = jnp.argsort(1 - mask_rows, axis=1, stable=True)[:, :key_most]
    live_slots = jnp.take_along_axis(mask_rows, key_order, axis=1) > 0
    return (key_order, live_slots)


def attend(
    query_units, blocks, key_slot, value_slot, key_lists, unit_heads, live_slots, unit_count
):
    unit_group = 4
    key_most = key_lists.shape[1]
    score_scale = 1.0 / math.sqrt(DH)
    out_init = jnp.zeros(query_units.shape, jnp.bfloat16)
    norm_init = jnp.zeros(query_units.shape[:2], jnp.float32)

    def one_turn(turn_index, loop_carry):
        outputs, lognorm = loop_carry
        first_unit = turn_index * unit_group
        group_queries = lax.dynamic_slice_in_dim(query_units, first_unit, unit_group, 0)
        group_rows = lax.dynamic_slice_in_dim(key_lists, first_unit, unit_group, 0)
        group_heads = lax.dynamic_slice_in_dim(unit_heads, first_unit, unit_group, 0)
        group_live = lax.dynamic_slice_in_dim(live_slots, first_unit, unit_group, 0)
        picked_keys = blocks[group_rows, :, group_heads[:, None], key_slot].reshape(
            unit_group, key_most * BLK, DH
        )
        picked_values = blocks[group_rows, :, group_heads[:, None], value_slot].reshape(
            unit_group, key_most * BLK, DH
        )
        scores = (
            jnp.einsum(
                "utc,ukc->utk", group_queries, picked_keys, preferred_element_type=jnp.float32
            )
            * score_scale
        )
        columns = jnp.repeat(group_live, BLK, axis=1)[:, None, :]
        masked = jnp.where(columns, scores, -jnp.inf)
        row_peak = jnp.max(masked, axis=2, keepdims=True)
        weights = jnp.where(columns, jnp.exp(masked - row_peak), 0.0)
        row_total = jnp.sum(weights, axis=2, keepdims=True)
        mixed_rows = (
            jnp.einsum(
                "utk,ukc->utc",
                weights.astype(jnp.bfloat16),
                picked_values,
                preferred_element_type=jnp.float32,
            )
            / row_total
        )
        outputs = lax.dynamic_update_slice_in_dim(
            outputs, mixed_rows.astype(jnp.bfloat16), first_unit, 0
        )
        lognorm = lax.dynamic_update_slice_in_dim(
            lognorm, (row_peak + jnp.log(row_total))[:, :, 0], first_unit, 0
        )
        return (outputs, lognorm)

    turn_total = (unit_count + unit_group - 1) // unit_group
    return lax.fori_loop(0, turn_total, one_turn, (out_init, norm_init))


def local(query_proj, key_proj, value_proj, block_mask, unit_plan, out_weight):
    tok_count = query_proj.shape[0]
    head_count = block_mask.shape[0]
    block_count = block_mask.shape[2]
    seq_count = lax.axis_size("seq")
    seq_index = lax.axis_index("seq")
    local_blocks = tok_count // BLK
    slab_most = min(2 * head_count * local_blocks, block_count)
    key_most = 2 * block_count // 5 + 1
    seq_tokens = seq_count * tok_count
    slab_units = -(-slab_most // 4) * 4
    owners = unit_plan[0, :, 0]
    firsts = unit_plan[0, :, 1]
    lengths = unit_plan[0, :, 2]
    own_head = owners[seq_index]
    own_first = firsts[seq_index]
    own_length = lengths[seq_index]
    query_local = query_proj.reshape(tok_count, head_count, DH)
    key_local = key_proj.reshape(tok_count, head_count, DH)
    value_local = value_proj.reshape(tok_count, head_count, DH)
    positions = seq_index * tok_count + jnp.arange(tok_count, dtype=jnp.int32)
    inside = (positions[None, :] >= firsts[:, None] * BLK) & (
        positions[None, :] < (firsts + lengths)[:, None] * BLK
    )
    filler = jnp.broadcast_to(
        (jnp.arange(block_count) == 0).astype(jnp.int32)[None, :], (slab_units, block_count)
    )
    sent_rows = by_owner(jnp.stack([key_local, value_local], axis=2), owners)
    arrived = lax.all_to_all(sent_rows, "seq", split_axis=0, concat_axis=0, tiled=True)
    blocks = arrived.reshape(block_count, BLK, 1, 2, DH)
    sent_queries = jnp.where(
        inside[:, :, None], by_owner(query_local, owners), jnp.zeros((), jnp.bfloat16)
    )
    head_queries = lax.all_to_all(
        sent_queries, "seq", split_axis=0, concat_axis=0, tiled=True
    ).reshape(seq_tokens, DH)
    key_slot = 0
    value_slot = 1
    head_queries = jnp.concatenate(
        [head_queries, jnp.zeros((slab_units * BLK, DH), jnp.bfloat16)], axis=0
    )
    query_units = lax.dynamic_slice_in_dim(
        head_queries, own_first * BLK, slab_units * BLK, 0
    ).reshape(slab_units, BLK, DH)
    head_mask = jnp.concatenate([block_mask[own_head], filler], axis=0)
    own_rows = lax.dynamic_slice_in_dim(head_mask, own_first, slab_units, 0)
    key_lists, live_slots = key_lists_of(own_rows, key_most)
    unit_heads = jnp.zeros((slab_units,), jnp.int32)
    outputs, lognorm = attend(
        query_units, blocks, key_slot, value_slot, key_lists, unit_heads, live_slots, own_length
    )
    unit_valid = jnp.arange(slab_units, dtype=jnp.int32) < own_length
    outputs = jnp.where(unit_valid[:, None, None], outputs, jnp.zeros((), jnp.bfloat16))
    unit_norm = jnp.where(unit_valid[:, None], lognorm, 0.0).reshape(slab_most * BLK)
    spread = jnp.zeros((seq_tokens + slab_units * BLK, DH), jnp.bfloat16)
    spread = lax.dynamic_update_slice_in_dim(
        spread, outputs.reshape(slab_units * BLK, DH), own_first * BLK, 0
    )
    returned = lax.all_to_all(
        spread[:seq_tokens].reshape(seq_count, tok_count, DH),
        "seq",
        split_axis=0,
        concat_axis=0,
        tiled=True,
    )
    head_picks = (owners[:, None] == jnp.arange(head_count, dtype=jnp.int32)[None, :]).astype(
        jnp.bfloat16
    )
    attn_local = (
        jnp.einsum("dh,dtc->thc", head_picks, returned, preferred_element_type=jnp.float32)
        .astype(jnp.bfloat16)
        .reshape(tok_count, head_count * DH)
    )
    summed = lax.psum_scatter(
        jnp.dot(attn_local, out_weight, preferred_element_type=jnp.float32),
        ("sub", "rep"),
        scatter_dimension=0,
        tiled=True,
    )
    return (summed.astype(jnp.bfloat16), unit_norm.reshape(1, 1, slab_most * BLK))


def solution(mesh):
    placed = (
        P(("grp", "seq"), ("sub", "rep")),
        P(("grp", "seq"), ("sub", "rep")),
        P(("grp", "seq"), ("sub", "rep")),
        P(("grp", "sub", "rep"), None, None),
        P(("grp", "sub", "rep"), None, None),
        P(("sub", "rep"), None),
    )
    return jax.shard_map(
        local,
        mesh=mesh,
        in_specs=placed,
        out_specs=(P(("grp", "seq", "sub", "rep"), None), P(("grp", "sub", "rep"), "seq", None)),
        check_vma=False,
    )
```

profile of v0, /device:TPU:0, one launch (start us, length us, event | category | flops | bytes accessed | tf_op | source)
XLA Modules:
  0.0 119.5 jit_solution(3339454133958437449)
XLA Ops:
  7.2 0.8 broadcast_compare_fusion.2
  8.0 0.7 slice_bitcast_fusion
  8.7 1.1 copy.52
  10.2 0.9 select_select_fusion.1
  11.2 6.3 %all-to-all-start = ((bf16[4,256,128]{2,1,0:T(8,128)(2,1)}), bf16[4,256,128]{2,1,0:T(8,128)(2,1)S(1)}, u32[]{:S(2)}, u32[]{:S(2)}) async-start(bf16[4,256,128]{2,1,0:T(8,128)(2,1)} %select_select_fusion.1), calls=%async_computation | async-start | bytes 524288 | tf_op jit(solution)/shard_map/all_to_all | solution.py:115
  17.5 1.1 copy.56
  25.8 0.7 dynamic-slice_bitcast_fusion
  26.5 0.9 select_select_fusion
  27.5 5.1 %all-to-all-start.1 = ((bf16[4,256,2,128]{3,1,2,0:T(8,128)(2,1)}), bf16[4,256,2,128]{3,1,2,0:T(8,128)(2,1)S(1)}, u32[]{:S(2)}, u32[]{:S(2)}) async-start(bf16[4,256,2,128]{3,1,2,0:T(8,128)(2,1)} %select_select_fusion), calls=%async_computation.1 | async-start | bytes 1048576 | tf_op jit(solution)/shard_map/all_to_all | solution.py:110
  34.3 0.7 iota_compare_fusion.1
  35.0 1.2 pad_dynamic-slice_fusion
  36.2 10.3 %all-to-all-done.1 = bf16[4,256,2,128]{3,1,2,0:T(8,128)(2,1)S(1)} async-done(((bf16[4,256,2,128]{3,1,2,0:T(8,128)(2,1)}), bf16[4,256,2,128]{3,1,2,0:T(8,128)(2,1)S(1)}, u32[]{:S(2)}, u32[]{:S(2)}) %all-to-all-start.1) | async-done | bytes 524320 | tf_op jit(solution)/shard_map/all_to_all | solution.py:110
  46.6 0.7 broadcast_in_dim.178
  47.3 11.1 %while.12 = (s32[]{:T(128)}, bf16[8,128,128]{2,1,0:T(8,128)(2,1)}, f32[8,128]{1,0:T(8,128)S(1)}, s32[]{:T(128)}, pred[8,4]{0,1:T(4,128)(4,1)S(1)}, /*index=5*/bf...) while((s32[]{:T(128)}, bf16[8,128,128]{2,1,0:T(8,128)(2,1)}, ...), condition=%wide.region_4.5_spmd, body=%wide.region_1.4_spmd.sunk | while | flops 136707680 | bytes 10778011 | solution.py:79
  48.6 1.4 %gather_fusion = bf16[16,128,128]{2,1,0:T(8,128)(2,1)} fusion(bf16[8,128,1,2,128]{4,1,3,2,0:T(8,128)(2,1)S(1)} %get-tuple-element.202, s32[16]{0:T(128)S(1)} %reshape.245), kind=kCustom, calls=%fused_computation.1.clone.1 | custom fusion | bytes 1048768 | tf_op jit(solution)/shard_map/while/body/gather | solution.py:47
  50.0 1.4 %fusion.41 = (f32[4,128]{1,0:T(4,128)S(1)}, f32[4,128,512]{2,1,0:T(8,128)S(1)}) fusion(bf16[4,512,128]{2,1,0:T(8,128)(2,1)S(1)} %bitcast.62, bf16[8,128,128]{2,1,0:T(8,128)(2,1)} %get-tuple-element.200, s32[]{:T(128)S(6)} %select_n.130, pred[4,512]{1,0:T(4,128)(4,1)S(1)} %bitcast.76), kind=kOutput, calls=%fused_computation.66.clone.1 | convolution fusion | flops 67894784 | bytes 1708036 | tf_op jit(solution)/shard_map/while/body/utc,ukc->utk/dot_general | solution.py:51
  54.2 1.4 %gather_fusion = bf16[16,128,128]{2,1,0:T(8,128)(2,1)} fusion(bf16[8,128,1,2,128]{4,1,3,2,0:T(8,128)(2,1)S(1)} %get-tuple-element.202, s32[16]{0:T(128)S(1)} %reshape.245), kind=kCustom, calls=%fused_computation.1.clone.1 | custom fusion | bytes 1048768 | tf_op jit(solution)/shard_map/while/body/gather | solution.py:47
  55.6 1.4 %fusion.41 = (f32[4,128]{1,0:T(4,128)S(1)}, f32[4,128,512]{2,1,0:T(8,128)S(1)}) fusion(bf16[4,512,128]{2,1,0:T(8,128)(2,1)S(1)} %bitcast.62, bf16[8,128,128]{2,1,0:T(8,128)(2,1)} %get-tuple-element.200, s32[]{:T(128)S(6)} %select_n.130, pred[4,512]{1,0:T(4,128)(4,1)S(1)} %bitcast.76), kind=kOutput, calls=%fused_computation.66.clone.1 | convolution fusion | flops 67894784 | bytes 1708036 | tf_op jit(solution)/shard_map/while/body/utc,ukc->utk/dot_general | solution.py:51
  57.7 0.7 copy-done.3
  58.4 1.0 broadcast_select_fusion
  59.6 10.8 %all_to_all.15 = bf16[4,256,128]{2,1,0:T(8,128)(2,1)S(1)} all-to-all(bf16[4,256,128]{2,1,0:T(8,128)(2,1)S(1)} %bitcast.68), channel_id=1, replica_groups=mesh['grp'=2,'seq'=4,'sub'=2,'rep'=2] {'seq'}, dimensions={0} | all-to-all | bytes 524288 | tf_op jit(solution)/shard_map/all_to_all | solution.py:140
  70.9 2.6 %fusion.25 = f32[256,3072]{1,0:T(8,128)} fusion(bf16[256,384]{0,1:T(8,128)(2,1)S(1)} %bitcast.69, bf16[384,3072]{1,0:T(8,128)(2,1)S(1)} %copy-done), kind=kOutput, calls=%fused_computation.68 | convolution fusion | flops 603979776 | bytes 5701632 | tf_op jit(solution)/shard_map/dot_general | solution.py:156
  74.3 36.5 %reduce-scatter.2.cloned.1.call-done = f32[64,3072]{1,0:T(8,128)} async-done(((f32[256,3072]{1,0:T(8,128)}), f32[64,3072]{1,0:T(8,128)}) %reduce-scatter.2.cloned.1.call-update) | async-done | bytes 786448 | tf_op jit(solution)/shard_map/reduce_scatter | solution.py:155
  110.7 1.9 %convert_element_type.26 = bf16[64,3072]{1,0:T(8,128)(2,1)} convert(f32[64,3072]{1,0:T(8,128)} %reduce-scatter.2.cloned.1.call-done) | non-fusion elementwise | flops 196608 | bytes 1179648 | tf_op jit(solution)/shard_map/convert_element_type | solution.py:161
  (80 shorter events, 10.2 us)
Async XLA Ops:
  7.2 63.8 %copy-start = (bf16[384,3072]{1,0:T(8,128)(2,1)S(1)}, bf16[384,3072]{1,0:T(8,128)(2,1)}, u32[]{:S(2)}) copy-start(bf16[384,3072]{1,0:T(8,128)(2,1)} %param.13) | copy-start | bytes 7077892
  7.2 11.4 %copy-start.4 = (bf16[256,384]{1,0:T(8,128)(2,1)S(1)}, bf16[256,384]{1,0:T(8,128)(2,1)}, u32[]{:S(2)}) copy-start(bf16[256,384]{1,0:T(8,128)(2,1)} %param.10) | copy-start | bytes 589828
  11.2 16.3 %all-to-all-start = ((bf16[4,256,128]{2,1,0:T(8,128)(2,1)}), bf16[4,256,128]{2,1,0:T(8,128)(2,1)S(1)}, u32[]{:S(2)}, u32[]{:S(2)}) async-start(bf16[4,256,128]{2,1,0:T(8,128)(2,1)} %select_select_fusion.1), calls=%async_computation | async-start | bytes 524288 | tf_op jit(solution)/shard_map/all_to_all | solution.py:115
  27.5 19.0 %all-to-all-start.1 = ((bf16[4,256,2,128]{3,1,2,0:T(8,128)(2,1)}), bf16[4,256,2,128]{3,1,2,0:T(8,128)(2,1)S(1)}, u32[]{:S(2)}, u32[]{:S(2)}) async-start(bf16[4,256,2,128]{3,1,2,0:T(8,128)(2,1)} %select_select_fusion), calls=%async_computation.1 | async-start | bytes 1048576 | tf_op jit(solution)/shard_map/all_to_all | solution.py:110
  32.6 78.2 %reduce-scatter.2.cloned.1.call-start = ((), (), s32[]{:S(2)}) async-start(), calls=%async_computation.4 | async-start | bytes 3932160 | tf_op jit(solution)/shard_map/reduce_scatter | solution.py:155
  50.0 1.7 %copy-start.1 = (bf16[16,128,128]{2,1,0:T(8,128)(2,1)S(1)}, bf16[16,128,128]{2,1,0:T(8,128)(2,1)}, u32[]{:S(2)}) copy-start(bf16[16,128,128]{2,1,0:T(8,128)(2,1)} %gather_fusion) | copy-start | bytes 1572868 | tf_op jit(solution)/shard_map/while
  50.0 1.7 %copy-start.2 = (bf16[8,128,128]{2,1,0:T(8,128)(2,1)S(1)}, bf16[8,128,128]{2,1,0:T(8,128)(2,1)}, u32[]{:S(2)}) copy-start(bf16[8,128,128]{2,1,0:T(8,128)(2,1)} %get-tuple-element.184) | copy-start | bytes 786436 | tf_op jit(solution)/shard_map/while
  52.2 0.7 copy-start.3
  55.6 1.7 %copy-start.1 = (bf16[16,128,128]{2,1,0:T(8,128)(2,1)S(1)}, bf16[16,128,128]{2,1,0:T(8,128)(2,1)}, u32[]{:S(2)}) copy-start(bf16[16,128,128]{2,1,0:T(8,128)(2,1)} %gather_fusion) | copy-start | bytes 1572868 | tf_op jit(solution)/shard_map/while
  55.6 1.7 %copy-start.2 = (bf16[8,128,128]{2,1,0:T(8,128)(2,1)S(1)}, bf16[8,128,128]{2,1,0:T(8,128)(2,1)}, u32[]{:S(2)}) copy-start(bf16[8,128,128]{2,1,0:T(8,128)(2,1)} %get-tuple-element.184) | copy-start | bytes 786436 | tf_op jit(solution)/shard_map/while
  57.7 0.7 copy-start.3
Sparse Core Ops, SparseCore 0:
  73.7 36.9 reduce-scatter.1
where the time goes:
time: 120 us
  waiting for transfers between devices  46.8 us (39%)
  between operations  19.6 us (16%)
  local copies, waits for them, and re-layouts  15.1 us (13%)
  starting transfers between devices  11.4 us (10%)
  blocking collectives  10.8 us (9%)
  other arithmetic  9.22 us (8%)
  matrix products  6.49 us (5%)
    reduce_scatter x1, waiting for transfers between devices, local(): lax.psum_scatter(jnp.dot(attn_local, out_weight, preferred_element_type=j...  36.5 us
    all_to_all x1, blocking collectives, local(): lax.all_to_all(spread[:seq_tokens].reshape(seq_count, tok_count, DH), 'se...  10.8 us
    all_to_all x1, waiting for transfers between devices, local(): lax.all_to_all(sent_rows, 'seq', split_axis=0, concat_axis=0, tiled=True)  10.3 us
    all_to_all x1, starting transfers between devices, local(): lax.all_to_all(sent_queries, 'seq', split_axis=0, concat_axis=0, tiled=True)  6.35 us
    all_to_all x1, starting transfers between devices, local(): lax.all_to_all(sent_rows, 'seq', split_axis=0, concat_axis=0, tiled=True)  5.09 us
    gather x2, local copies, waits for them, and re-layouts, one_turn(): blocks[group_rows, :, group_heads[:, None], value_slot]  2.83 us
    dot_general x2, matrix products, one_turn(): jnp.einsum('utc,ukc->utk', group_queries, picked_keys, preferred_element_...  2.71 us
    dot_general x1, matrix products, local(): jnp.dot(attn_local, out_weight, preferred_element_type=jnp.float32)  2.65 us
  transfers between devices with their start and end apart: 3, of which 2 were waited for; matrix products, arithmetic and copies ran while one was open for 7% of the time, Pallas kernels for 0%

commit v1 on v0

--- a/solution.py
+++ b/solution.py
@@ -153,12 +153,12 @@
         .reshape(tok_count, head_count * DH)
     )
     summed = lax.psum_scatter(
-        jnp.dot(attn_local, out_weight, preferred_element_type=jnp.float32),
+        jnp.dot(attn_local, out_weight, preferred_element_type=jnp.float32).astype(jnp.bfloat16),
         ("sub", "rep"),
         scatter_dimension=0,
         tiled=True,
     )
-    return (summed.astype(jnp.bfloat16), unit_norm.reshape(1, 1, slab_most * BLK))
+    return (summed, unit_norm.reshape(1, 1, slab_most * BLK))
 
 
 def solution(mesh):

time: 120 us -> 115 us (0.958)
  waiting for transfers between devices: 46.8 us -> 37 us
  local copies, waits for them, and re-layouts: 15.1 us -> 20.2 us
  matrix products: 6.49 us -> 9.58 us
  other arithmetic: 9.22 us -> 7.25 us
    reduce_scatter x1, waiting for transfers between devices: 36.5 us -> 27.3 us  [local(): lax.psum_scatter(jnp.dot(attn_local, out_weight, preferred_element_type=j...]
    gather x2, local copies, waits for them, and re-layouts: 1.31 us -> 4.89 us  [one_turn(): blocks[group_rows, :, group_heads[:, None], key_slot]]
    dot_general x2, matrix products: 0.84 us -> 4.13 us  [one_turn(): jnp.einsum('utk,ukc->utc', weights.astype(jnp.bfloat16), picked_values, p...]
    gather x2, local copies, waits for them, and re-layouts: 2.83 us -> 4.9 us  [one_turn(): blocks[group_rows, :, group_heads[:, None], value_slot]]
    convert_element_type x1 -> x0, other arithmetic: 1.92 us -> none  [local(): summed.astype(jnp.bfloat16)]
    while x16 -> x4, local copies, waits for them, and re-layouts: 1.55 us -> 0.17 us
  transfers between devices with their start and end apart: 3 -> 3, of which waited for: 2 -> 2; matrix products, arithmetic and copies ran while one was open for 7% -> 8% of each run, Pallas kernels for 0% -> 0%
where the time goes in v1:
time: 115 us
  waiting for transfers between devices  37 us (32%)
  local copies, waits for them, and re-layouts  20.2 us (18%)
  between operations  19.3 us (17%)
  starting transfers between devices  11.4 us (10%)
  blocking collectives  10.2 us (9%)
  matrix products  9.58 us (8%)
  other arithmetic  7.25 us (6%)
    reduce_scatter x1, waiting for transfers between devices, local(): lax.psum_scatter(jnp.dot(attn_local, out_weight, preferred_element_type=j...  27.3 us
    all_to_all x1, blocking collectives, local(): lax.all_to_all(spread[:seq_tokens].reshape(seq_count, tok_count, DH), 'se...  10.2 us
    all_to_all x1, waiting for transfers between devices, local(): lax.all_to_all(sent_rows, 'seq', split_axis=0, concat_axis=0, tiled=True)  9.66 us
    all_to_all x1, starting transfers between devices, local(): lax.all_to_all(sent_queries, 'seq', split_axis=0, concat_axis=0, tiled=True)  6.35 us
    all_to_all x1, starting transfers between devices, local(): lax.all_to_all(sent_rows, 'seq', split_axis=0, concat_axis=0, tiled=True)  5.09 us
    gather x2, local copies, waits for them, and re-layouts, one_turn(): blocks[group_rows, :, group_heads[:, None], value_slot]  4.9 us
    gather x2, local copies, waits for them, and re-layouts, one_turn(): blocks[group_rows, :, group_heads[:, None], key_slot]  4.89 us
    dot_general x2, matrix products, one_turn(): jnp.einsum('utk,ukc->utc', weights.astype(jnp.bfloat16), picked_values, p...  4.13 us
  transfers between devices with their start and end apart: 3, of which 2 were waited for; matrix products, arithmetic and copies ran while one was open for 8% of the time, Pallas kernels for 0%

profile of v1, /device:TPU:0, one launch (start us, length us, event | category | flops | bytes accessed | tf_op | source)
XLA Modules:
  0.0 114.9 jit_solution(6250197844109399266)
XLA Ops:
  7.2 0.9 slice_bitcast_fusion
  8.7 1.1 copy.52
  10.3 0.9 select_select_fusion.1
  11.2 6.3 %all-to-all-start = ((bf16[4,256,128]{2,1,0:T(8,128)(2,1)}), bf16[4,256,128]{2,1,0:T(8,128)(2,1)S(1)}, u32[]{:S(2)}, u32[]{:S(2)}) async-start(bf16[4,256,128]{2,1,0:T(8,128)(2,1)} %select_select_fusion.1), calls=%async_computation | async-start | bytes 524288 | tf_op jit(solution)/shard_map/all_to_all | solution.py:115
  17.5 1.1 copy.56
  25.6 0.9 select_select_fusion
  26.5 5.1 %all-to-all-start.1 = ((bf16[4,256,2,128]{3,1,2,0:T(8,128)(2,1)}), bf16[4,256,2,128]{3,1,2,0:T(8,128)(2,1)S(1)}, u32[]{:S(2)}, u32[]{:S(2)}) async-start(bf16[4,256,2,128]{3,1,2,0:T(8,128)(2,1)} %select_select_fusion), calls=%async_computation.1 | async-start | bytes 1048576 | tf_op jit(solution)/shard_map/all_to_all | solution.py:110
  34.7 1.2 %pad_dynamic-slice_fusion = bf16[1024,128]{1,0:T(8,128)(2,1)} fusion(s32[]{:T(128)S(6)} %select_n.88, bf16[1024,128]{1,0:T(8,128)(2,1)S(1)} %bitcast.67), kind=kLoop, calls=%fused_computation.30 | loop fusion | bytes 524292 | tf_op jit(solution)/shard_map/dynamic_slice | solution.py:123
  35.9 9.7 %all-to-all-done.1 = bf16[4,256,2,128]{3,1,2,0:T(8,128)(2,1)S(1)} async-done(((bf16[4,256,2,128]{3,1,2,0:T(8,128)(2,1)}), bf16[4,256,2,128]{3,1,2,0:T(8,128)(2,1)S(1)}, u32[]{:S(2)}, u32[]{:S(2)}) %all-to-all-start.1) | async-done | bytes 524320 | tf_op jit(solution)/shard_map/all_to_all | solution.py:110
  45.6 0.8 copy.64
  46.4 0.7 broadcast_in_dim.178
  47.1 18.9 %while.12 = (s32[]{:T(128)}, bf16[8,128,128]{2,1,0:T(8,128)(2,1)}, f32[8,128]{1,0:T(8,128)S(1)}, s32[]{:T(128)}, pred[8,4]{0,1:T(4,128)(4,1)S(1)}, /*index=5*/bf...) while((s32[]{:T(128)}, bf16[8,128,128]{2,1,0:T(8,128)(2,1)}, ...), condition=%wide.region_4.5_spmd, body=%wide.region_1.4_spmd.sunk | while | flops 136707680 | bytes 6583623 | solution.py:79
  47.4 2.4 %gather_fusion.1 = bf16[16,128,128]{2,1,0:T(8,128)(2,1)} fusion(bf16[8,128,1,2,128]{4,1,3,2,0:T(8,128)(2,1)} %get-tuple-element.202, s32[16]{0:T(128)S(1)} %reshape.246), kind=kCustom, calls=%fused_computation.clone.1 | custom fusion | bytes 1048768 | tf_op jit(solution)/shard_map/while/body/gather | solution.py:44
  50.1 1.5 %fusion.40 = (f32[4,128]{1,0:T(4,128)S(1)}, f32[4,128,512]{2,1,0:T(8,128)S(1)}) fusion(bf16[4,512,128]{2,1,0:T(8,128)(2,1)} %bitcast.62, bf16[8,128,128]{2,1,0:T(8,128)(2,1)} %get-tuple-element.200, s32[]{:T(128)S(6)} %select_n.130, pred[4,512]{1,0:T(4,128)(4,1)S(1)} %bitcast.76), kind=kOutput, calls=%fused_computation.67.clone.1 | convolution fusion | flops 67894784 | bytes 1708036 | tf_op jit(solution)/shard_map/while/body/utc,ukc->utk/dot_general | solution.py:51
  52.1 2.5 %gather_fusion = bf16[16,128,128]{2,1,0:T(8,128)(2,1)} fusion(bf16[8,128,1,2,128]{4,1,3,2,0:T(8,128)(2,1)} %get-tuple-element.202, s32[16]{0:T(128)S(1)} %reshape.245), kind=kCustom, calls=%fused_computation.1.clone.1 | custom fusion | bytes 1048768 | tf_op jit(solution)/shard_map/while/body/gather | solution.py:47
  54.5 2.1 %fusion.42 = bf16[8,128,128]{2,1,0:T(8,128)(2,1)} fusion(bf16[8,128,128]{2,1,0:T(8,128)(2,1)} %get-tuple-element.184, s32[]{:T(128)S(6)} %select_n.130, bf16[4,512,128]{2,1,0:T(8,128)(2,1)} %bitcast.63, f32[4,128,512]{2,1,0:T(8,128)S(1)} %get-tuple-element.169, f32[4,128]{1,0:T(4,128)S(1)} %get-tuple-element.170, pred[4,512]{1,0:T(4,128)(4,1)S(1)} %bitcast.78, ...), kind=kOutput, calls=%fused_computation.7.clone.1 | convolution fusion | flops 68026368 | bytes 1710084 | tf_op jit(solution)/shard_map/while/body/utk,ukc->utc/dot_general | solution.py:62
  56.8 2.4 %gather_fusion.1 = bf16[16,128,128]{2,1,0:T(8,128)(2,1)} fusion(bf16[8,128,1,2,128]{4,1,3,2,0:T(8,128)(2,1)} %get-tuple-element.202, s32[16]{0:T(128)S(1)} %reshape.246), kind=kCustom, calls=%fused_computation.clone.1 | custom fusion | bytes 1048768 | tf_op jit(solution)/shard_map/while/body/gather | solution.py:44
  59.6 1.5 %fusion.40 = (f32[4,128]{1,0:T(4,128)S(1)}, f32[4,128,512]{2,1,0:T(8,128)S(1)}) fusion(bf16[4,512,128]{2,1,0:T(8,128)(2,1)} %bitcast.62, bf16[8,128,128]{2,1,0:T(8,128)(2,1)} %get-tuple-element.200, s32[]{:T(128)S(6)} %select_n.130, pred[4,512]{1,0:T(4,128)(4,1)S(1)} %bitcast.76), kind=kOutput, calls=%fused_computation.67.clone.1 | convolution fusion | flops 67894784 | bytes 1708036 | tf_op jit(solution)/shard_map/while/body/utc,ukc->utk/dot_general | solution.py:51
  61.5 2.5 %gather_fusion = bf16[16,128,128]{2,1,0:T(8,128)(2,1)} fusion(bf16[8,128,1,2,128]{4,1,3,2,0:T(8,128)(2,1)} %get-tuple-element.202, s32[16]{0:T(128)S(1)} %reshape.245), kind=kCustom, calls=%fused_computation.1.clone.1 | custom fusion | bytes 1048768 | tf_op jit(solution)/shard_map/while/body/gather | solution.py:47
  63.9 2.1 %fusion.42 = bf16[8,128,128]{2,1,0:T(8,128)(2,1)} fusion(bf16[8,128,128]{2,1,0:T(8,128)(2,1)} %get-tuple-element.184, s32[]{:T(128)S(6)} %select_n.130, bf16[4,512,128]{2,1,0:T(8,128)(2,1)} %bitcast.63, f32[4,128,512]{2,1,0:T(8,128)S(1)} %get-tuple-element.169, f32[4,128]{1,0:T(4,128)S(1)} %get-tuple-element.170, pred[4,512]{1,0:T(4,128)(4,1)S(1)} %bitcast.78, ...), kind=kOutput, calls=%fused_computation.7.clone.1 | convolution fusion | flops 68026368 | bytes 1710084 | tf_op jit(solution)/shard_map/while/body/utk,ukc->utc/dot_general | solution.py:62
  66.0 1.0 broadcast_select_fusion
  67.2 10.2 %all_to_all.15 = bf16[4,256,128]{2,1,0:T(8,128)(2,1)S(1)} all-to-all(bf16[4,256,128]{2,1,0:T(8,128)(2,1)S(1)} %bitcast.68), channel_id=1, replica_groups=mesh['grp'=2,'seq'=4,'sub'=2,'rep'=2] {'seq'}, dimensions={0} | all-to-all | bytes 524288 | tf_op jit(solution)/shard_map/all_to_all | solution.py:140
  77.9 2.2 %convolution_convert_fusion = bf16[256,3072]{1,0:T(8,128)(2,1)} fusion(bf16[256,384]{0,1:T(8,128)(2,1)S(1)} %bitcast.69, bf16[384,3072]{1,0:T(8,128)(2,1)S(1)} %copy-done), kind=kOutput, calls=%fused_computation.26 | convolution fusion | flops 604766208 | bytes 4128768 | tf_op jit(solution)/shard_map/dot_general | solution.py:156
  80.7 27.3 %reduce-scatter.2.cloned.1.call-done = bf16[64,3072]{1,0:T(8,128)(2,1)} async-done(((bf16[256,3072]{1,0:T(8,128)(2,1)}), bf16[64,3072]{1,0:T(8,128)(2,1)}) %reduce-scatter.2.cloned.1.call-update) | async-done | bytes 393232 | tf_op jit(solution)/shard_map/reduce_scatter | solution.py:155
  (67 shorter events, 9.3 us)
Async XLA Ops:
  7.2 70.7 %copy-start = (bf16[384,3072]{1,0:T(8,128)(2,1)S(1)}, bf16[384,3072]{1,0:T(8,128)(2,1)}, u32[]{:S(2)}) copy-start(bf16[384,3072]{1,0:T(8,128)(2,1)} %param.13) | copy-start | bytes 7077892
  7.2 11.4 %copy-start.1 = (bf16[256,384]{1,0:T(8,128)(2,1)S(1)}, bf16[256,384]{1,0:T(8,128)(2,1)}, u32[]{:S(2)}) copy-start(bf16[256,384]{1,0:T(8,128)(2,1)} %param.10) | copy-start | bytes 589828
  11.2 15.3 %all-to-all-start = ((bf16[4,256,128]{2,1,0:T(8,128)(2,1)}), bf16[4,256,128]{2,1,0:T(8,128)(2,1)S(1)}, u32[]{:S(2)}, u32[]{:S(2)}) async-start(bf16[4,256,128]{2,1,0:T(8,128)(2,1)} %select_select_fusion.1), calls=%async_computation | async-start | bytes 524288 | tf_op jit(solution)/shard_map/all_to_all | solution.py:115
  26.5 19.0 %all-to-all-start.1 = ((bf16[4,256,2,128]{3,1,2,0:T(8,128)(2,1)}), bf16[4,256,2,128]{3,1,2,0:T(8,128)(2,1)S(1)}, u32[]{:S(2)}, u32[]{:S(2)}) async-start(bf16[4,256,2,128]{3,1,2,0:T(8,128)(2,1)} %select_select_fusion), calls=%async_computation.1 | async-start | bytes 1048576 | tf_op jit(solution)/shard_map/all_to_all | solution.py:110
  31.6 76.4 %reduce-scatter.2.cloned.1.call-start = ((), (), s32[]{:S(2)}) async-start(), calls=%async_computation.4 | async-start | bytes 1966080 | tf_op jit(solution)/shard_map/reduce_scatter | solution.py:155
Sparse Core Ops, SparseCore 0:
  80.2 27.7 reduce-scatter.1

commit v2 on v1

v2 whole, which is shorter than its diff:
```python
import math

import jax
import jax.numpy as jnp
from jax import lax
from jax.sharding import PartitionSpec as P

DH = 128
BLK = 128


def local(query_proj, key_proj, value_proj, block_mask, unit_plan, out_weight):
    tok_count = query_proj.shape[0]
    head_count = block_mask.shape[0]
    block_count = block_mask.shape[2]
    seq_index = lax.axis_index("seq")
    local_blocks = tok_count // BLK
    slab_most = min(2 * head_count * local_blocks, block_count)
    score_scale = 1.0 / math.sqrt(DH)
    key_value = jnp.stack([key_proj, value_proj], axis=0)
    gathered = lax.all_gather(key_value, "seq", axis=1, tiled=True)
    all_tokens = gathered.shape[1]
    keys = gathered[0].reshape(all_tokens, head_count, DH)
    values = gathered[1].reshape(all_tokens, head_count, DH)
    queries = query_proj.reshape(tok_count, head_count, DH)
    scores = (
        jnp.einsum("thc,shc->hts", queries, keys, preferred_element_type=jnp.float32)
        * score_scale
    )
    own_rows = lax.dynamic_slice_in_dim(block_mask, seq_index * local_blocks, local_blocks, 1)
    live = jnp.repeat(jnp.repeat(own_rows > 0, BLK, axis=1), BLK, axis=2)
    masked = jnp.where(live, scores, -jnp.inf)
    row_peak = jnp.max(masked, axis=2, keepdims=True)
    weights = jnp.where(live, jnp.exp(masked - row_peak), 0.0)
    row_total = jnp.sum(weights, axis=2, keepdims=True)
    mixed = (
        jnp.einsum(
            "hts,shc->htc",
            weights.astype(jnp.bfloat16),
            values,
            preferred_element_type=jnp.float32,
        )
        / row_total
    )
    attn_local = mixed.astype(jnp.bfloat16).transpose(1, 0, 2).reshape(tok_count, head_count * DH)
    lognorm = (row_peak + jnp.log(row_total))[:, :, 0]
    all_norm = lax.all_gather(lognorm, "seq", axis=1, tiled=True)
    own_head = unit_plan[0, seq_index, 0]
    own_first = unit_plan[0, seq_index, 1]
    own_length = unit_plan[0, seq_index, 2]
    head_norm = jnp.concatenate(
        [all_norm[own_head], jnp.zeros((slab_most * BLK,), jnp.float32)], axis=0
    )
    unit_norm = lax.dynamic_slice_in_dim(head_norm, own_first * BLK, slab_most * BLK, 0)
    unit_norm = jnp.where(
        jnp.arange(slab_most * BLK, dtype=jnp.int32) < own_length * BLK, unit_norm, 0.0
    )
    summed = lax.psum_scatter(
        jnp.dot(attn_local, out_weight, preferred_element_type=jnp.float32).astype(jnp.bfloat16),
        ("sub", "rep"),
        scatter_dimension=0,
        tiled=True,
    )
    return (summed, unit_norm.reshape(1, 1, slab_most * BLK))


def solution(mesh):
    placed = (
        P(("grp", "seq"), ("sub", "rep")),
        P(("grp", "seq"), ("sub", "rep")),
        P(("grp", "seq"), ("sub", "rep")),
        P(("grp", "sub", "rep"), None, None),
        P(("grp", "sub", "rep"), None, None),
        P(("sub", "rep"), None),
    )
    return jax.shard_map(
        local,
        mesh=mesh,
        in_specs=placed,
        out_specs=(P(("grp", "seq", "sub", "rep"), None), P(("grp", "sub", "rep"), "seq", None)),
        check_vma=False,
    )
```

time: 115 us -> 90.1 us (0.78)
  local copies, waits for them, and re-layouts: 20.2 us -> 5.6 us
  starting transfers between devices: 11.4 us -> 0.08 us
  waiting for transfers between devices: 37 us -> 47.5 us
  matrix products: 9.58 us -> 3.21 us
  other arithmetic: 7.25 us -> 3.03 us
  blocking collectives: 10.2 us -> 13.2 us
  between operations: 19.3 us -> 17.1 us
    all_gather x0 -> x1, waiting for transfers between devices: none -> 38.6 us  [local(): gathered = lax.all_gather(key_value, 'seq', axis=1, tiled=True)]
    reduce_scatter x1, waiting for transfers between devices: 27.3 us -> 8.86 us  [local(): lax.psum_scatter(jnp.dot(attn_local, out_weight, preferred_element_type=j...]
    all_gather x0 -> x1, blocking collectives: none -> 13.2 us  [local(): all_norm = lax.all_gather(lognorm, 'seq', axis=1, tiled=True)]
    all_to_all x2 -> x0, starting transfers between devices: 11.4 us -> none  [the longest x1 6.35 us: local(): lax.all_to_all(sent_queries, 'seq', split_axis=0, concat_axis=0, tiled=True)]
    gather x9 -> x0, local copies, waits for them, and re-layouts: 10.8 us -> none  [the longest x2 4.9 us: one_turn(): blocks[group_rows, :, group_heads[:, None], value_slot]]
    all_to_all x1 -> x0, blocking collectives: 10.2 us -> none  [local(): lax.all_to_all(spread[:seq_tokens].reshape(seq_count, tok_count, DH), 'se...]
    all_to_all x2 -> x0, waiting for transfers between devices: 9.66 us -> none  [the longest x1 9.66 us: local(): lax.all_to_all(sent_rows, 'seq', split_axis=0, concat_axis=0, tiled=True)]
    dot_general x5 -> x2, matrix products: 7.42 us -> 1.03 us  [the longest x1 0.66 us: local(): jnp.einsum('thc,shc->hts', queries, keys, preferred_element_type=jnp.floa...]
  transfers between devices with their start and end apart: 3 -> 2, of which waited for: 2 -> 2; matrix products, arithmetic and copies ran while one was open for 8% -> 4% of each run, Pallas kernels for 0% -> 0%
where the time goes in v2:
time: 90.1 us; the launch traced here: 89.8 us
  waiting for transfers between devices  47.5 us (53%)
  between operations  17.1 us (19%)
  blocking collectives  13.2 us (15%)
  local copies, waits for them, and re-layouts  5.6 us (6%)
  matrix products  3.21 us (4%)
  other arithmetic  3.03 us (3%)
    all_gather x1, waiting for transfers between devices, local(): gathered = lax.all_gather(key_value, 'seq', axis=1, tiled=True)  38.6 us
    all_gather x1, blocking collectives, local(): all_norm = lax.all_gather(lognorm, 'seq', axis=1, tiled=True)  13.2 us
    reduce_scatter x1, waiting for transfers between devices, local(): lax.psum_scatter(jnp.dot(attn_local, out_weight, preferred_element_type=j...  8.86 us
    unnamed x7, local copies, waits for them, and re-layouts  3.35 us
    dot_general x1, matrix products, local(): jnp.dot(attn_local, out_weight, preferred_element_type=jnp.float32)  2.18 us
  transfers between devices with their start and end apart: 2, of which 2 were waited for; matrix products, arithmetic and copies ran while one was open for 4% of the time, Pallas kernels for 0%

profile of v2, /device:TPU:0, one launch (start us, length us, event | category | flops | bytes accessed | tf_op | source)
XLA Modules:
  0.0 89.8 jit_solution(11464944111205112207)
XLA Ops:
  7.2 0.0 copy-start
  7.2 0.0 all-gather.2.cloned.1.call-start
  7.2 1.2 %copy.12 = bf16[256,384]{0,1:T(8,128)(2,1)S(1)} copy(bf16[256,384]{1,0:T(8,128)(2,1)} %param.8) | data formatting | bytes 393216 | tf_op args[2]
  8.4 1.1 %copy.11 = bf16[256,384]{0,1:T(8,128)(2,1)S(1)} copy(bf16[256,384]{1,0:T(8,128)(2,1)} %param.7) | data formatting | bytes 393216 | tf_op args[1]
  9.5 0.8 pad_maximum_fusion
  10.3 0.0 all-gather.2.cloned.1.call-update
  10.3 0.0 reduce-scatter.2.cloned.1.call-start
  10.4 1.1 %copy.13 = bf16[256,384]{0,1:T(8,128)(2,1)S(1)} copy(bf16[256,384]{1,0:T(8,128)(2,1)} %param.6) | data formatting | bytes 393216 | tf_op args[0]
  11.4 0.7 dynamic-slice_compare_fusion
  12.2 0.1 broadcast_bitcast_fusion
  12.2 38.6 %all-gather.2.cloned.1.call-done = bf16[2,1024,384]{1,2,0:T(8,128)(2,1)} async-done(((bf16[2,256,384]{1,2,0:T(8,128)(2,1)}), bf16[2,1024,384]{1,2,0:T(8,128)(2,1)}) %all-gather.2.cloned.1.call-update) | async-done | bytes 1572880 | tf_op jit(solution)/shard_map/all_gather | solution.py:21
  50.9 1.5 %fusion.6 = (bf16[1,1024,384]{1,2,0:T(8,128)(2,1)S(1)}, bf16[1,1024,384]{1,2,0:T(8,128)(2,1)S(1)}) fusion(bf16[2,1024,384]{1,2,0:T(8,128)(2,1)} %all-gather.2.cloned.1.call-done), kind=kLoop, calls=%fused_computation.20 | loop fusion | bytes 3145728 | tf_op jit(solution)/shard_map/slice | solution.py:23
  52.4 0.7 fusion
  53.0 0.8 fusion.1
  53.9 0.4 fusion.4
  54.3 0.0 copy-start.1
  54.3 0.0 copy-done
  54.3 2.2 %convolution_convert_fusion = bf16[256,3072]{1,0:T(8,128)(2,1)} fusion(bf16[256,384]{0,1:T(8,128)(2,1)S(1)} %bitcast.52, bf16[384,3072]{1,0:T(8,128)(2,1)S(1)} %copy-done), kind=kOutput, calls=%fused_computation.2 | convolution fusion | flops 604766208 | bytes 4128768 | tf_op jit(solution)/shard_map/dot_general | solution.py:59
  56.5 0.0 reduce-scatter.2.cloned.1.call-update
  56.5 0.0 copy-done.1
  56.5 0.7 constant_dynamic-slice_fusion.3
  60.2 13.2 %all_gather.7 = f32[3,1024]{1,0:T(4,128)S(1)} all-gather(f32[3,256]{1,0:T(4,128)S(1)} %log_add_fusion), channel_id=1, replica_groups=mesh['grp'=2,'seq'=4,'sub'=2,'rep'=2] {'seq'}, dimensions={1}, use_global_device_ids=true | all-gather | bytes 15360 | tf_op jit(solution)/shard_map/all_gather | solution.py:47
  73.4 0.7 fusion.5
  74.1 8.9 %reduce-scatter.2.cloned.1.call-done = bf16[64,3072]{1,0:T(8,128)(2,1)} async-done(((bf16[256,3072]{1,0:T(8,128)(2,1)}), bf16[64,3072]{1,0:T(8,128)(2,1)}) %reduce-scatter.2.cloned.1.call-update) | async-done | bytes 393232 | tf_op jit(solution)/shard_map/reduce_scatter | solution.py:58
  (2 shorter events, 0.0 us)
Async XLA Ops:
  7.2 47.1 %copy-start = (bf16[384,3072]{1,0:T(8,128)(2,1)S(1)}, bf16[384,3072]{1,0:T(8,128)(2,1)}, u32[]{:S(2)}) copy-start(bf16[384,3072]{1,0:T(8,128)(2,1)} %param.11) | copy-start | bytes 7077892
  7.2 43.7 %all-gather.2.cloned.1.call-start = ((), (), s32[]{:S(2)}) async-start(), calls=%async_computation.1 | async-start | bytes 1966080 | tf_op jit(solution)/shard_map/all_gather | solution.py:21
  10.3 72.6 %reduce-scatter.2.cloned.1.call-start = ((), (), s32[]{:S(2)}) async-start(), calls=%async_computation.2 | async-start | bytes 1966080 | tf_op jit(solution)/shard_map/reduce_scatter | solution.py:58
  54.3 2.2 %copy-start.1 = (s32[1,4,3]{1,0,2:T(1,128)S(1)}, s32[1,4,3]{1,0,2:T(1,128)}, u32[]{:S(2)}) copy-start(s32[1,4,3]{1,0,2:T(1,128)} %param.10) | copy-start | bytes 148
Sparse Core Ops, SparseCore 0:
  10.4 40.3 all-gather.1
  56.6 26.2 reduce-scatter.1

commit v3 on v2

--- a/solution.py
+++ b/solution.py
@@ -9,6 +9,14 @@
 BLK = 128
 
 
+def around(piece, count):
+    pieces = [piece]
+    for shift in range(1, count):
+        pairs = [(source, (source + shift) % count) for source in range(count)]
+        pieces.append(lax.ppermute(piece, "seq", pairs))
+    return pieces
+
+
 def local(query_proj, key_proj, value_proj, block_mask, unit_plan, out_weight):
     tok_count = query_proj.shape[0]
     head_count = block_mask.shape[0]
@@ -17,9 +25,12 @@
     local_blocks = tok_count // BLK
     slab_most = min(2 * head_count * local_blocks, block_count)
     score_scale = 1.0 / math.sqrt(DH)
+    seq_count = lax.axis_size("seq")
     key_value = jnp.stack([key_proj, value_proj], axis=0)
-    gathered = lax.all_gather(key_value, "seq", axis=1, tiled=True)
+    gathered = jnp.concatenate(around(key_value, seq_count), axis=1)
     all_tokens = gathered.shape[1]
+    sources = (seq_index - jnp.arange(seq_count, dtype=jnp.int32)) % seq_count
+    column_order = (sources[:, None] * local_blocks + jnp.arange(local_blocks)[None, :]).reshape(-1)
     keys = gathered[0].reshape(all_tokens, head_count, DH)
     values = gathered[1].reshape(all_tokens, head_count, DH)
     queries = query_proj.reshape(tok_count, head_count, DH)
@@ -28,6 +39,7 @@
         * score_scale
     )
     own_rows = lax.dynamic_slice_in_dim(block_mask, seq_index * local_blocks, local_blocks, 1)
+    own_rows = jnp.take(own_rows, column_order, axis=2)
     live = jnp.repeat(jnp.repeat(own_rows > 0, BLK, axis=1), BLK, axis=2)
     masked = jnp.where(live, scores, -jnp.inf)
     row_peak = jnp.max(masked, axis=2, keepdims=True)
@@ -44,7 +56,9 @@
     )
     attn_local = mixed.astype(jnp.bfloat16).transpose(1, 0, 2).reshape(tok_count, head_count * DH)
     lognorm = (row_peak + jnp.log(row_total))[:, :, 0]
-    all_norm = lax.all_gather(lognorm, "seq", axis=1, tiled=True)
+    arrived = jnp.stack(around(lognorm, seq_count), axis=0)
+    all_norm = jnp.take(arrived, (seq_index - jnp.arange(seq_count)) % seq_count, axis=0)
+    all_norm = all_norm.transpose(1, 0, 2).reshape(head_count, seq_count * tok_count)
     own_head = unit_plan[0, seq_index, 0]
     own_first = unit_plan[0, seq_index, 1]
     own_length = unit_plan[0, seq_index, 2]

time: 90.1 us -> 90.6 us (level)
  blocking collectives: 13.2 us -> 0 us
  starting transfers between devices: 0.08 us -> 11 us
    all_gather x1 -> x0, waiting for transfers between devices: 38.6 us -> none  [local(): gathered = lax.all_gather(key_value, 'seq', axis=1, tiled=True)]
    ppermute x0 -> x6, waiting for transfers between devices: none -> 29.8 us  [around(): pieces.append(lax.ppermute(piece, 'seq', pairs))]
    all_gather x1 -> x0, blocking collectives: 13.2 us -> none  [local(): all_norm = lax.all_gather(lognorm, 'seq', axis=1, tiled=True)]
    ppermute x0 -> x6, starting transfers between devices: none -> 11 us  [around(): pieces.append(lax.ppermute(piece, 'seq', pairs))]
    reduce_scatter x1, waiting for transfers between devices: 8.86 us -> 18.5 us  [local(): lax.psum_scatter(jnp.dot(attn_local, out_weight, preferred_element_type=j...]
    slice x1, local copies, waits for them, and re-layouts: 1.49 us -> 0.12 us  [local(): keys = gathered[0].reshape(all_tokens, head_count, DH)]
    concatenate x0 -> x1, other arithmetic: none -> 1.31 us  [local(): gathered = jnp.concatenate(around(key_value, seq_count), axis=1)]
    gather x0 -> x2, local copies, waits for them, and re-layouts: none -> 1.15 us  [the longest x1 0.58 us: local(): own_rows = jnp.take(own_rows, column_order, axis=2)]
  transfers between devices with their start and end apart: 2 -> 7, of which waited for: 2 -> 3; matrix products, arithmetic and copies ran while one was open for 4% -> 6% of each run, Pallas kernels for 0% -> 0%
where the time goes in v3:
time: 90.6 us; the launch traced here: 90.3 us
  waiting for transfers between devices  48.3 us (53%)
  between operations  17.4 us (19%)
  starting transfers between devices  11 us (12%)
  local copies, waits for them, and re-layouts  6.46 us (7%)
  other arithmetic  3.91 us (4%)
  matrix products  3.2 us (4%)
    ppermute x6, waiting for transfers between devices, around(): pieces.append(lax.ppermute(piece, 'seq', pairs))  29.8 us
    reduce_scatter x1, waiting for transfers between devices, local(): lax.psum_scatter(jnp.dot(attn_local, out_weight, preferred_element_type=j...  18.5 us
    ppermute x6, starting transfers between devices, around(): pieces.append(lax.ppermute(piece, 'seq', pairs))  11 us
    unnamed x8, local copies, waits for them, and re-layouts  3.45 us
    dot_general x1, matrix products, local(): jnp.dot(attn_local, out_weight, preferred_element_type=jnp.float32)  2.16 us
  transfers between devices with their start and end apart: 7, of which 3 were waited for; matrix products, arithmetic and copies ran while one was open for 6% of the time, Pallas kernels for 0%

profile of v3, /device:TPU:0, one launch (start us, length us, event | category | flops | bytes accessed | tf_op | source)
XLA Modules:
  0.0 90.3 jit_solution(13559782511733516342)
XLA Ops:
  7.2 1.2 %copy.14 = bf16[256,384]{0,1:T(8,128)(2,1)S(1)} copy(bf16[256,384]{1,0:T(8,128)(2,1)} %param.8) | data formatting | bytes 393216 | tf_op args[2]
  8.4 1.1 %copy.13 = bf16[256,384]{0,1:T(8,128)(2,1)S(1)} copy(bf16[256,384]{1,0:T(8,128)(2,1)} %param.7) | data formatting | bytes 393216 | tf_op args[1]
  9.5 0.8 pad_maximum_fusion.1
  10.3 5.1 %collective-permute-start.2 = (bf16[2,256,384]{1,2,0:T(8,128)(2,1)}, bf16[2,256,384]{1,2,0:T(8,128)(2,1)S(1)}, u32[]{:S(2)}, u32[]{:S(2)}) collective-permute-start(bf16[2,256,384]{1,2,0:T(8,128)(2,1)} %pad_maximum_fusion.1), channel_id=1, source_target_pairs={{0,12},{4,0},{8,4},{12,8},{1,13},{5,1},{9,5},{13,9},{2,14},{6,2},{... | collective-permute-start | bytes 1179656 | tf_op jit(solution)/shard_map/ppermute | solution.py:16
  15.4 1.0 %collective-permute-start = (bf16[2,256,384]{1,2,0:T(8,128)(2,1)}, bf16[2,256,384]{1,2,0:T(8,128)(2,1)}, u32[]{:S(2)}, u32[]{:S(2)}) collective-permute-start(bf16[2,256,384]{1,2,0:T(8,128)(2,1)} %pad_maximum_fusion.1), channel_id=1, source_target_pairs={{0,4},{4,8},{8,12},{12,0},{1,5},{5,9},{9,13},{13,1},{2,6},{6,10},{... | collective-permute-start | bytes 1179656 | tf_op jit(solution)/shard_map/ppermute | solution.py:16
  16.6 0.7 constant_dynamic-slice_fusion.4
  17.4 0.1 copy.22
  17.5 0.6 gather_fusion
  18.1 0.1 copy.12
  18.3 1.1 %copy.15 = bf16[256,384]{0,1:T(8,128)(2,1)S(1)} copy(bf16[256,384]{1,0:T(8,128)(2,1)} %param.6) | data formatting | bytes 393216 | tf_op args[0]
  19.4 5.8 %collective-permute-done.2 = bf16[2,256,384]{1,2,0:T(8,128)(2,1)S(1)} collective-permute-done((bf16[2,256,384]{1,2,0:T(8,128)(2,1)}, bf16[2,256,384]{1,2,0:T(8,128)(2,1)S(1)}, u32[]{:S(2)}, u32[]{:S(2)}) %collective-permute-start.2) | collective-permute-done | bytes 393248 | tf_op jit(solution)/shard_map/ppermute | solution.py:16
  25.2 24.0 %collective-permute-done.1 = bf16[2,256,384]{1,2,0:T(8,128)(2,1)} collective-permute-done((bf16[2,256,384]{1,2,0:T(8,128)(2,1)}, bf16[2,256,384]{1,2,0:T(8,128)(2,1)}, u32[]{:S(2)}, u32[]{:S(2)}) %collective-permute-start.1) | collective-permute-done | bytes 393248 | tf_op jit(solution)/shard_map/ppermute | solution.py:16
  49.2 1.3 %pad_maximum_fusion = bf16[2,1024,384]{1,2,0:T(8,128)(2,1)S(1)} fusion(bf16[2,256,384]{1,2,0:T(8,128)(2,1)S(1)} %collective-permute-done.2, bf16[2,256,384]{1,2,0:T(8,128)(2,1)} %collective-permute-done.1, bf16[2,256,384]{1,2,0:T(8,128)(2,1)} %collective-permute-done, bf16[1,256,384]{1,2,0:T(8,128)(2,1)S(1)} %bitcast.62, bf16[1,256,384]{1,2,0:T(8,128)(2,1)S(1)} %bitcast.64), kind=kLoop, calls=%fused_computation.8 | loop fusion | flops 7864320 | bytes 3145728 | tf_op jit(solution)/shard_map/concatenate | solution.py:30
  50.6 0.1 fusion.10
  50.7 0.7 fusion
  51.3 0.8 fusion.1
  52.2 0.4 fusion.4
  52.6 2.2 %convolution_convert_fusion = bf16[256,3072]{1,0:T(8,128)(2,1)} fusion(bf16[256,384]{0,1:T(8,128)(2,1)S(1)} %bitcast.67, bf16[384,3072]{1,0:T(8,128)(2,1)S(1)} %copy-done), kind=kOutput, calls=%fused_computation.4 | convolution fusion | flops 604766208 | bytes 4128768 | tf_op jit(solution)/shard_map/dot_general | solution.py:73
  54.9 2.9 %collective-permute-start.4 = (f32[3,256]{1,0:T(4,128)S(1)}, f32[3,256]{1,0:T(4,128)S(1)}, u32[]{:S(2)}, u32[]{:S(2)}) collective-permute-start(f32[3,256]{1,0:T(4,128)S(1)} %log_add_fusion), channel_id=1, source_target_pairs={{0,8},{4,12},{8,0},{12,4},{1,9},{5,13},{9,1},{13,5},{2,10},{6,14},... | collective-permute-start | bytes 9224 | tf_op jit(solution)/shard_map/ppermute | solution.py:16
  57.8 1.9 %collective-permute-start.3 = (f32[3,256]{1,0:T(4,128)S(1)}, f32[3,256]{1,0:T(4,128)S(1)}, u32[]{:S(2)}, u32[]{:S(2)}) collective-permute-start(f32[3,256]{1,0:T(4,128)S(1)} %log_add_fusion), channel_id=1, source_target_pairs={{0,4},{4,8},{8,12},{12,0},{1,5},{5,9},{9,13},{13,1},{2,6},{6,10},{... | collective-permute-start | bytes 9224 | tf_op jit(solution)/shard_map/ppermute | solution.py:16
  59.7 0.7 constant_dynamic-slice_fusion.3
  63.6 0.6 gather_fusion.1
  64.3 0.7 fusion.5
  65.0 18.5 %reduce-scatter.2.cloned.1.call-done = bf16[64,3072]{1,0:T(8,128)(2,1)} async-done(((bf16[256,3072]{1,0:T(8,128)(2,1)}), bf16[64,3072]{1,0:T(8,128)(2,1)}) %reduce-scatter.2.cloned.1.call-update) | async-done | bytes 393232 | tf_op jit(solution)/shard_map/reduce_scatter | solution.py:72
  (28 shorter events, 0.7 us)
Async XLA Ops:
  7.2 45.4 %copy-start = (bf16[384,3072]{1,0:T(8,128)(2,1)S(1)}, bf16[384,3072]{1,0:T(8,128)(2,1)}, u32[]{:S(2)}) copy-start(bf16[384,3072]{1,0:T(8,128)(2,1)} %param.11) | copy-start | bytes 7077892
  7.2 76.2 %reduce-scatter.2.cloned.1.call-start = ((), (), s32[]{:S(2)}) async-start(), calls=%async_computation.1 | async-start | bytes 1966080 | tf_op jit(solution)/shard_map/reduce_scatter | solution.py:72
  10.3 14.9 %collective-permute-start.2 = (bf16[2,256,384]{1,2,0:T(8,128)(2,1)}, bf16[2,256,384]{1,2,0:T(8,128)(2,1)S(1)}, u32[]{:S(2)}, u32[]{:S(2)}) collective-permute-start(bf16[2,256,384]{1,2,0:T(8,128)(2,1)} %pad_maximum_fusion.1), channel_id=1, source_target_pairs={{0,12},{4,0},{8,4},{12,8},{1,13},{5,1},{9,5},{13,9},{2,14},{6,2},{... | collective-permute-start | bytes 1179656 | tf_op jit(solution)/shard_map/ppermute | solution.py:16
  15.4 33.9 %collective-permute-start.1 = (bf16[2,256,384]{1,2,0:T(8,128)(2,1)}, bf16[2,256,384]{1,2,0:T(8,128)(2,1)}, u32[]{:S(2)}, u32[]{:S(2)}) collective-permute-start(bf16[2,256,384]{1,2,0:T(8,128)(2,1)} %pad_maximum_fusion.1), channel_id=1, source_target_pairs={{0,8},{4,12},{8,0},{12,4},{1,9},{5,13},{9,1},{13,5},{2,10},{6,14},... | collective-permute-start | bytes 1179656 | tf_op jit(solution)/shard_map/ppermute | solution.py:16
  15.4 33.9 %collective-permute-start = (bf16[2,256,384]{1,2,0:T(8,128)(2,1)}, bf16[2,256,384]{1,2,0:T(8,128)(2,1)}, u32[]{:S(2)}, u32[]{:S(2)}) collective-permute-start(bf16[2,256,384]{1,2,0:T(8,128)(2,1)} %pad_maximum_fusion.1), channel_id=1, source_target_pairs={{0,4},{4,8},{8,12},{12,0},{1,5},{5,9},{9,13},{13,1},{2,6},{6,10},{... | collective-permute-start | bytes 1179656 | tf_op jit(solution)/shard_map/ppermute | solution.py:16
  52.6 7.2 %copy-start.1 = (s32[1,4,3]{1,0,2:T(1,128)S(1)}, s32[1,4,3]{1,0,2:T(1,128)}, u32[]{:S(2)}) copy-start(s32[1,4,3]{1,0,2:T(1,128)} %param.10) | copy-start | bytes 148
  54.8 8.8 %collective-permute-start.5 = (f32[3,256]{1,0:T(4,128)S(1)}, f32[3,256]{1,0:T(4,128)S(1)}, u32[]{:S(2)}, u32[]{:S(2)}) collective-permute-start(f32[3,256]{1,0:T(4,128)S(1)} %log_add_fusion), channel_id=1, source_target_pairs={{0,12},{4,0},{8,4},{12,8},{1,13},{5,1},{9,5},{13,9},{2,14},{6,2},{... | collective-permute-start | bytes 9224 | tf_op jit(solution)/shard_map/ppermute | solution.py:16
  54.9 8.7 %collective-permute-start.4 = (f32[3,256]{1,0:T(4,128)S(1)}, f32[3,256]{1,0:T(4,128)S(1)}, u32[]{:S(2)}, u32[]{:S(2)}) collective-permute-start(f32[3,256]{1,0:T(4,128)S(1)} %log_add_fusion), channel_id=1, source_target_pairs={{0,8},{4,12},{8,0},{12,4},{1,9},{5,13},{9,1},{13,5},{2,10},{6,14},... | collective-permute-start | bytes 9224 | tf_op jit(solution)/shard_map/ppermute | solution.py:16
  57.8 5.9 %collective-permute-start.3 = (f32[3,256]{1,0:T(4,128)S(1)}, f32[3,256]{1,0:T(4,128)S(1)}, u32[]{:S(2)}, u32[]{:S(2)}) collective-permute-start(f32[3,256]{1,0:T(4,128)S(1)} %log_add_fusion), channel_id=1, source_target_pairs={{0,4},{4,8},{8,12},{12,0},{1,5},{5,9},{9,13},{13,1},{2,6},{6,10},{... | collective-permute-start | bytes 9224 | tf_op jit(solution)/shard_map/ppermute | solution.py:16
Sparse Core Ops, SparseCore 0:
  54.9 28.4 reduce-scatter.1

commit v4 on v3

--- a/solution.py
+++ b/solution.py
@@ -69,12 +69,15 @@
     unit_norm = jnp.where(
         jnp.arange(slab_most * BLK, dtype=jnp.int32) < own_length * BLK, unit_norm, 0.0
     )
-    summed = lax.psum_scatter(
-        jnp.dot(attn_local, out_weight, preferred_element_type=jnp.float32).astype(jnp.bfloat16),
-        ("sub", "rep"),
-        scatter_dimension=0,
-        tiled=True,
+    partial = jnp.dot(attn_local, out_weight, preferred_element_type=jnp.float32)
+    sub_count = lax.axis_size("sub")
+    rep_count = lax.axis_size("rep")
+    partial = partial.astype(jnp.bfloat16).reshape(
+        sub_count, rep_count, tok_count // (sub_count * rep_count), partial.shape[1]
     )
+    partial = lax.psum_scatter(partial.transpose(1, 0, 2, 3), "rep", scatter_dimension=0, tiled=True)
+    summed = lax.psum_scatter(partial, "sub", scatter_dimension=1, tiled=True)
+    summed = summed.reshape(summed.shape[0] * summed.shape[1] * summed.shape[2], summed.shape[3])
     return (summed, unit_norm.reshape(1, 1, slab_most * BLK))
 
 

time: 90.6 us -> 93.3 us (1.030)
  waiting for transfers between devices: 48.3 us -> 50.8 us
  local copies, waits for them, and re-layouts: 6.46 us -> 7.73 us
  matrix products: 3.2 us -> 2.04 us
    reduce_scatter x1 -> x2, waiting for transfers between devices: 18.5 us -> 20.6 us  [the longest x1 11.1 us: local(): summed = lax.psum_scatter(partial, 'sub', scatter_dimension=1, tiled=True)]
    reshape x0 -> x1, local copies, waits for them, and re-layouts: none -> 1.26 us  [local(): partial.astype(jnp.bfloat16)]
    dot_general x1, matrix products: 2.16 us -> 1.01 us  [local(): jnp.dot(attn_local, out_weight, preferred_element_type=jnp.float32)]
  transfers between devices with their start and end apart: 7 -> 8, of which waited for: 3 -> 5; matrix products, arithmetic and copies ran while one was open for 6% -> 5% of each run, Pallas kernels for 0% -> 0%
where the time goes in v4:
time: 93.3 us; the launch traced here: 93 us
  waiting for transfers between devices  50.8 us (54%)
  between operations  17.5 us (19%)
  starting transfers between devices  11 us (12%)
  local copies, waits for them, and re-layouts  7.73 us (8%)
  other arithmetic  3.91 us (4%)
  matrix products  2.04 us (2%)
    ppermute x6, waiting for transfers between devices, around(): pieces.append(lax.ppermute(piece, 'seq', pairs))  30.1 us
    reduce_scatter x1, waiting for transfers between devices, local(): summed = lax.psum_scatter(partial, 'sub', scatter_dimension=1, tiled=True)  11.1 us
    ppermute x6, starting transfers between devices, around(): pieces.append(lax.ppermute(piece, 'seq', pairs))  10.9 us
    reduce_scatter x1, waiting for transfers between devices, local(): lax.psum_scatter(partial.transpose(1, 0, 2, 3), 'rep', scatter_dimension=...  9.59 us
    unnamed x8, local copies, waits for them, and re-layouts  3.45 us
  transfers between devices with their start and end apart: 8, of which 5 were waited for; matrix products, arithmetic and copies ran while one was open for 5% of the time, Pallas kernels for 0%

profile of v4, /device:TPU:0, one launch (start us, length us, event | category | flops | bytes accessed | tf_op | source)
XLA Modules:
  0.0 93.0 jit_solution(7840761610242388001)
XLA Ops:
  7.2 1.2 %copy.15 = bf16[256,384]{0,1:T(8,128)(2,1)S(1)} copy(bf16[256,384]{1,0:T(8,128)(2,1)} %param.8) | data formatting | bytes 393216 | tf_op args[2]
  8.4 1.1 %copy.14 = bf16[256,384]{0,1:T(8,128)(2,1)S(1)} copy(bf16[256,384]{1,0:T(8,128)(2,1)} %param.7) | data formatting | bytes 393216 | tf_op args[1]
  9.5 0.8 pad_maximum_fusion.1
  10.3 5.1 %collective-permute-start.2 = (bf16[2,256,384]{1,2,0:T(8,128)(2,1)}, bf16[2,256,384]{1,2,0:T(8,128)(2,1)S(1)}, u32[]{:S(2)}, u32[]{:S(2)}) collective-permute-start(bf16[2,256,384]{1,2,0:T(8,128)(2,1)} %pad_maximum_fusion.1), channel_id=1, source_target_pairs={{0,12},{4,0},{8,4},{12,8},{1,13},{5,1},{9,5},{13,9},{2,14},{6,2},{... | collective-permute-start | bytes 1179656 | tf_op jit(solution)/shard_map/ppermute | solution.py:16
  15.4 1.0 %collective-permute-start = (bf16[2,256,384]{1,2,0:T(8,128)(2,1)}, bf16[2,256,384]{1,2,0:T(8,128)(2,1)}, u32[]{:S(2)}, u32[]{:S(2)}) collective-permute-start(bf16[2,256,384]{1,2,0:T(8,128)(2,1)} %pad_maximum_fusion.1), channel_id=1, source_target_pairs={{0,4},{4,8},{8,12},{12,0},{1,5},{5,9},{9,13},{13,1},{2,6},{6,10},{... | collective-permute-start | bytes 1179656 | tf_op jit(solution)/shard_map/ppermute | solution.py:16
  16.6 0.7 constant_dynamic-slice_fusion.4
  17.5 0.6 gather_fusion
  18.3 1.1 %copy.16 = bf16[256,384]{0,1:T(8,128)(2,1)S(1)} copy(bf16[256,384]{1,0:T(8,128)(2,1)} %param.6) | data formatting | bytes 393216 | tf_op args[0]
  19.4 5.8 %collective-permute-done.2 = bf16[2,256,384]{1,2,0:T(8,128)(2,1)S(1)} collective-permute-done((bf16[2,256,384]{1,2,0:T(8,128)(2,1)}, bf16[2,256,384]{1,2,0:T(8,128)(2,1)S(1)}, u32[]{:S(2)}, u32[]{:S(2)}) %collective-permute-start.2) | collective-permute-done | bytes 393248 | tf_op jit(solution)/shard_map/ppermute | solution.py:16
  25.2 24.0 %collective-permute-done.1 = bf16[2,256,384]{1,2,0:T(8,128)(2,1)} collective-permute-done((bf16[2,256,384]{1,2,0:T(8,128)(2,1)}, bf16[2,256,384]{1,2,0:T(8,128)(2,1)}, u32[]{:S(2)}, u32[]{:S(2)}) %collective-permute-start.1) | collective-permute-done | bytes 393248 | tf_op jit(solution)/shard_map/ppermute | solution.py:16
  49.2 1.3 %pad_maximum_fusion = bf16[2,1024,384]{1,2,0:T(8,128)(2,1)S(1)} fusion(bf16[2,256,384]{1,2,0:T(8,128)(2,1)S(1)} %collective-permute-done.2, bf16[2,256,384]{1,2,0:T(8,128)(2,1)} %collective-permute-done.1, bf16[2,256,384]{1,2,0:T(8,128)(2,1)} %collective-permute-done, bf16[1,256,384]{1,2,0:T(8,128)(2,1)S(1)} %bitcast.69, bf16[1,256,384]{1,2,0:T(8,128)(2,1)S(1)} %bitcast.71), kind=kLoop, calls=%fused_computation.8 | loop fusion | flops 7864320 | bytes 3145728 | tf_op jit(solution)/shard_map/concatenate | solution.py:30
  50.7 0.7 fusion
  51.3 0.8 fusion.1
  52.2 0.4 fusion.4
  52.6 1.0 %convolution_convert_fusion = bf16[256,3072]{1,0:T(8,128)(2,1)S(1)} fusion(bf16[256,384]{0,1:T(8,128)(2,1)S(1)} %bitcast.74, bf16[384,3072]{1,0:T(8,128)(2,1)S(1)} %copy-done), kind=kOutput, calls=%fused_computation.4 | convolution fusion | flops 604766208 | bytes 4128768 | tf_op jit(solution)/shard_map/dot_general | solution.py:72
  53.6 1.3 %copy.26 = bf16[2,2,64,3072]{3,2,0,1:T(8,128)(2,1)} copy(bf16[2,2,64,3072]{3,2,1,0:T(8,128)(2,1)S(1)} %bitcast.66) | data formatting | bytes 3145728 | tf_op jit(solution)/shard_map/reshape | solution.py:75
  54.9 9.6 %reduce-scatter.3.cloned.1.call-done = bf16[1,2,64,3072]{3,2,1,0:T(8,128)(2,1)} async-done(((bf16[2,2,64,3072]{3,2,1,0:T(8,128)(2,1)}), bf16[1,2,64,3072]{3,2,1,0:T(8,128)(2,1)}) %reduce-scatter.3.cloned.1.call-update) | async-done | bytes 786448 | tf_op jit(solution)/shard_map/reduce_scatter | solution.py:78
  64.6 3.7 %collective-permute-start.5 = (f32[3,256]{1,0:T(4,128)S(1)}, f32[3,256]{1,0:T(4,128)S(1)}, u32[]{:S(2)}, u32[]{:S(2)}) collective-permute-start(f32[3,256]{1,0:T(4,128)S(1)} %log_add_fusion), channel_id=1, source_target_pairs={{0,12},{4,0},{8,4},{12,8},{1,13},{5,1},{9,5},{13,9},{2,14},{6,2},{... | collective-permute-start | bytes 9224 | tf_op jit(solution)/shard_map/ppermute | solution.py:16
  68.3 1.1 %collective-permute-start.3 = (f32[3,256]{1,0:T(4,128)S(1)}, f32[3,256]{1,0:T(4,128)S(1)}, u32[]{:S(2)}, u32[]{:S(2)}) collective-permute-start(f32[3,256]{1,0:T(4,128)S(1)} %log_add_fusion), channel_id=1, source_target_pairs={{0,4},{4,8},{8,12},{12,0},{1,5},{5,9},{9,13},{13,1},{2,6},{6,10},{... | collective-permute-start | bytes 9224 | tf_op jit(solution)/shard_map/ppermute | solution.py:16
  69.5 0.7 constant_dynamic-slice_fusion.3
  73.4 0.3 collective-permute-done.3
  73.7 0.6 gather_fusion.1
  74.4 0.7 fusion.5
  75.1 11.1 %reduce-scatter.5.cloned.1.call-done = bf16[1,1,64,3072]{3,2,1,0:T(8,128)(2,1)} async-done(((bf16[1,2,64,3072]{3,2,1,0:T(8,128)(2,1)}), bf16[1,1,64,3072]{3,2,1,0:T(8,128)(2,1)}) %reduce-scatter.5.cloned.1.call-update) | async-done | bytes 393232 | tf_op jit(solution)/shard_map/reduce_scatter | solution.py:79
  (32 shorter events, 1.0 us)
Async XLA Ops:
  7.2 45.4 %copy-start = (bf16[384,3072]{1,0:T(8,128)(2,1)S(1)}, bf16[384,3072]{1,0:T(8,128)(2,1)}, u32[]{:S(2)}) copy-start(bf16[384,3072]{1,0:T(8,128)(2,1)} %param.11) | copy-start | bytes 7077892
  7.2 57.3 %reduce-scatter.3.cloned.1.call-start = ((), (), s32[]{:S(2)}) async-start(), calls=%async_computation.2 | async-start | bytes 2359296 | tf_op jit(solution)/shard_map/reduce_scatter | solution.py:78
  10.3 14.9 %collective-permute-start.2 = (bf16[2,256,384]{1,2,0:T(8,128)(2,1)}, bf16[2,256,384]{1,2,0:T(8,128)(2,1)S(1)}, u32[]{:S(2)}, u32[]{:S(2)}) collective-permute-start(bf16[2,256,384]{1,2,0:T(8,128)(2,1)} %pad_maximum_fusion.1), channel_id=1, source_target_pairs={{0,12},{4,0},{8,4},{12,8},{1,13},{5,1},{9,5},{13,9},{2,14},{6,2},{... | collective-permute-start | bytes 1179656 | tf_op jit(solution)/shard_map/ppermute | solution.py:16
  15.4 33.9 %collective-permute-start.1 = (bf16[2,256,384]{1,2,0:T(8,128)(2,1)}, bf16[2,256,384]{1,2,0:T(8,128)(2,1)}, u32[]{:S(2)}, u32[]{:S(2)}) collective-permute-start(bf16[2,256,384]{1,2,0:T(8,128)(2,1)} %pad_maximum_fusion.1), channel_id=1, source_target_pairs={{0,8},{4,12},{8,0},{12,4},{1,9},{5,13},{9,1},{13,5},{2,10},{6,14},... | collective-permute-start | bytes 1179656 | tf_op jit(solution)/shard_map/ppermute | solution.py:16
  15.4 33.9 %collective-permute-start = (bf16[2,256,384]{1,2,0:T(8,128)(2,1)}, bf16[2,256,384]{1,2,0:T(8,128)(2,1)}, u32[]{:S(2)}, u32[]{:S(2)}) collective-permute-start(bf16[2,256,384]{1,2,0:T(8,128)(2,1)} %pad_maximum_fusion.1), channel_id=1, source_target_pairs={{0,4},{4,8},{8,12},{12,0},{1,5},{5,9},{9,13},{13,1},{2,6},{6,10},{... | collective-permute-start | bytes 1179656 | tf_op jit(solution)/shard_map/ppermute | solution.py:16
  53.6 15.9 %copy-start.1 = (s32[1,4,3]{1,0,2:T(1,128)S(1)}, s32[1,4,3]{1,0,2:T(1,128)}, u32[]{:S(2)}) copy-start(s32[1,4,3]{1,0,2:T(1,128)} %param.10) | copy-start | bytes 148
  54.9 31.3 %reduce-scatter.5.cloned.1.call-start = ((), (), s32[]{:S(2)}) async-start(), calls=%async_computation.3 | async-start | bytes 1179648 | tf_op jit(solution)/shard_map/reduce_scatter | solution.py:79
  64.6 8.8 %collective-permute-start.5 = (f32[3,256]{1,0:T(4,128)S(1)}, f32[3,256]{1,0:T(4,128)S(1)}, u32[]{:S(2)}, u32[]{:S(2)}) collective-permute-start(f32[3,256]{1,0:T(4,128)S(1)} %log_add_fusion), channel_id=1, source_target_pairs={{0,12},{4,0},{8,4},{12,8},{1,13},{5,1},{9,5},{13,9},{2,14},{6,2},{... | collective-permute-start | bytes 9224 | tf_op jit(solution)/shard_map/ppermute | solution.py:16
  68.3 5.1 %collective-permute-start.4 = (f32[3,256]{1,0:T(4,128)S(1)}, f32[3,256]{1,0:T(4,128)S(1)}, u32[]{:S(2)}, u32[]{:S(2)}) collective-permute-start(f32[3,256]{1,0:T(4,128)S(1)} %log_add_fusion), channel_id=1, source_target_pairs={{0,8},{4,12},{8,0},{12,4},{1,9},{5,13},{9,1},{13,5},{2,10},{6,14},... | collective-permute-start | bytes 9224 | tf_op jit(solution)/shard_map/ppermute | solution.py:16
  68.3 5.4 %collective-permute-start.3 = (f32[3,256]{1,0:T(4,128)S(1)}, f32[3,256]{1,0:T(4,128)S(1)}, u32[]{:S(2)}, u32[]{:S(2)}) collective-permute-start(f32[3,256]{1,0:T(4,128)S(1)} %log_add_fusion), channel_id=1, source_target_pairs={{0,4},{4,8},{8,12},{12,0},{1,5},{5,9},{9,13},{13,1},{2,6},{6,10},{... | collective-permute-start | bytes 9224 | tf_op jit(solution)/shard_map/ppermute | solution.py:16
Sparse Core Ops, SparseCore 0:
  55.0 9.4 reduce-scatter.2
  67.3 18.7 reduce-scatter.4

commit v5 on v4

--- a/solution.py
+++ b/solution.py
@@ -70,15 +70,17 @@
         jnp.arange(slab_most * BLK, dtype=jnp.int32) < own_length * BLK, unit_norm, 0.0
     )
     partial = jnp.dot(attn_local, out_weight, preferred_element_type=jnp.float32)
-    sub_count = lax.axis_size("sub")
     rep_count = lax.axis_size("rep")
-    partial = partial.astype(jnp.bfloat16).reshape(
-        sub_count, rep_count, tok_count // (sub_count * rep_count), partial.shape[1]
-    )
-    partial = lax.psum_scatter(partial.transpose(1, 0, 2, 3), "rep", scatter_dimension=0, tiled=True)
-    summed = lax.psum_scatter(partial, "sub", scatter_dimension=1, tiled=True)
-    summed = summed.reshape(summed.shape[0] * summed.shape[1] * summed.shape[2], summed.shape[3])
-    return (summed, unit_norm.reshape(1, 1, slab_most * BLK))
+    peer_count = lax.axis_size("sub") * rep_count
+    peer_index = lax.axis_index("sub") * rep_count + lax.axis_index("rep")
+    chunk = tok_count // peer_count
+    chunks = partial.astype(jnp.bfloat16).reshape(peer_count, chunk, partial.shape[1])
+    summed = partial.reshape(peer_count, chunk, partial.shape[1])[peer_index]
+    for shift in range(1, peer_count):
+        pairs = [(source, (source + shift) % peer_count) for source in range(peer_count)]
+        sent = chunks[(peer_index + shift) % peer_count]
+        summed = summed + lax.ppermute(sent, ("sub", "rep"), pairs).astype(jnp.float32)
+    return (summed.astype(jnp.bfloat16), unit_norm.reshape(1, 1, slab_most * BLK))
 
 
 def solution(mesh):

time: 93.3 us -> 77.2 us (0.83)
  between operations: 17.5 us -> 3.91 us
  waiting for transfers between devices: 50.8 us -> 38.3 us
  other arithmetic: 3.91 us -> 8.07 us
  starting transfers between devices: 11 us -> 14.2 us
  matrix products: 2.04 us -> 3.7 us
    reduce_scatter x2 -> x0, waiting for transfers between devices: 20.6 us -> none  [the longest x1 11.1 us: local(): summed = lax.psum_scatter(partial, 'sub', scatter_dimension=1, tiled=True)]
    ppermute x0 -> x3, waiting for transfers between devices: none -> 14.1 us  [local(): lax.ppermute(sent, ('sub', 'rep'), pairs).astype(jnp.float32)]
    ppermute x6, waiting for transfers between devices: 30.1 us -> 24.2 us  [around(): pieces.append(lax.ppermute(piece, 'seq', pairs))]
    ppermute x0 -> x3, starting transfers between devices: none -> 3.24 us  [local(): lax.ppermute(sent, ('sub', 'rep'), pairs).astype(jnp.float32)]
    convert_element_type x0 -> x1, other arithmetic: none -> 2.29 us  [local(): summed.astype(jnp.bfloat16)]
    dot_general x1, matrix products: 1.01 us -> 2.64 us  [local(): jnp.dot(attn_local, out_weight, preferred_element_type=jnp.float32)]
    reshape x1 -> x0, local copies, waits for them, and re-layouts: 1.26 us -> none  [local(): partial.astype(jnp.bfloat16)]
    unnamed x8 -> x6, local copies, waits for them, and re-layouts: 3.45 us -> 3.44 us
  transfers between devices with their start and end apart: 8 -> 9, of which waited for: 5 -> 5; matrix products, arithmetic and copies ran while one was open for 5% -> 16% of each run, Pallas kernels for 0% -> 0%
where the time goes in v5:
time: 77.2 us; the launch traced here: 76.8 us
  waiting for transfers between devices  38.3 us (50%)
  starting transfers between devices  14.2 us (18%)
  local copies, waits for them, and re-layouts  8.65 us (11%)
  other arithmetic  8.07 us (10%)
  between operations  3.91 us (5%)
  matrix products  3.7 us (5%)
    ppermute x6, waiting for transfers between devices, around(): pieces.append(lax.ppermute(piece, 'seq', pairs))  24.2 us
    ppermute x3, waiting for transfers between devices, local(): lax.ppermute(sent, ('sub', 'rep'), pairs).astype(jnp.float32)  14.1 us
    ppermute x6, starting transfers between devices, around(): pieces.append(lax.ppermute(piece, 'seq', pairs))  10.9 us
    unnamed x6, local copies, waits for them, and re-layouts  3.44 us
    ppermute x3, starting transfers between devices, local(): lax.ppermute(sent, ('sub', 'rep'), pairs).astype(jnp.float32)  3.24 us
    dot_general x1, matrix products, local(): jnp.dot(attn_local, out_weight, preferred_element_type=jnp.float32)  2.64 us
    convert_element_type x1, other arithmetic, local(): summed.astype(jnp.bfloat16)  2.29 us
  transfers between devices with their start and end apart: 9, of which 5 were waited for; matrix products, arithmetic and copies ran while one was open for 16% of the time, Pallas kernels for 0%

profile of v5, /device:TPU:0, one launch (start us, length us, event | category | flops | bytes accessed | tf_op | source)
XLA Modules:
  0.0 76.8 jit_solution(15589973159356548549)
XLA Ops:
  0.6 1.2 %copy.13 = bf16[256,384]{0,1:T(8,128)(2,1)S(1)} copy(bf16[256,384]{1,0:T(8,128)(2,1)} %param.7) | data formatting | bytes 393216 | tf_op args[1]
  1.9 1.1 %copy.14 = bf16[256,384]{0,1:T(8,128)(2,1)S(1)} copy(bf16[256,384]{1,0:T(8,128)(2,1)} %param.8) | data formatting | bytes 393216 | tf_op args[2]
  2.9 0.8 %pad_maximum_fusion.1 = bf16[2,256,384]{1,2,0:T(8,128)(2,1)} fusion(bf16[1,256,384]{1,2,0:T(8,128)(2,1)S(1)} %bitcast.81, bf16[1,256,384]{1,2,0:T(8,128)(2,1)S(1)} %bitcast.79), kind=kLoop, calls=%fused_computation.15 | loop fusion | flops 196608 | bytes 786432 | tf_op jit(solution)/shard_map/stack | solution.py:29
  3.7 5.1 %collective-permute-start.2 = (bf16[2,256,384]{1,2,0:T(8,128)(2,1)}, bf16[2,256,384]{1,2,0:T(8,128)(2,1)S(1)}, u32[]{:S(2)}, u32[]{:S(2)}) collective-permute-start(bf16[2,256,384]{1,2,0:T(8,128)(2,1)} %pad_maximum_fusion.1), channel_id=1, source_target_pairs={{0,12},{4,0},{8,4},{12,8},{1,13},{5,1},{9,5},{13,9},{2,14},{6,2},{... | collective-permute-start | bytes 1179656 | tf_op jit(solution)/shard_map/ppermute | solution.py:16
  8.8 1.0 %collective-permute-start = (bf16[2,256,384]{1,2,0:T(8,128)(2,1)}, bf16[2,256,384]{1,2,0:T(8,128)(2,1)}, u32[]{:S(2)}, u32[]{:S(2)}) collective-permute-start(bf16[2,256,384]{1,2,0:T(8,128)(2,1)} %pad_maximum_fusion.1), channel_id=1, source_target_pairs={{0,4},{4,8},{8,12},{12,0},{1,5},{5,9},{9,13},{13,1},{2,6},{6,10},{... | collective-permute-start | bytes 1179656 | tf_op jit(solution)/shard_map/ppermute | solution.py:16
  10.4 1.3 %constant_dynamic-slice_fusion.3 = (s32[1,1,1]{1,0,2:T(1,128)}, s32[1,1,1]{1,0,2:T(1,128)}, s32[1,1,1]{1,0,2:T(1,128)}) fusion(s32[1,4,3]{1,0,2:T(1,128)} %param.10, s32[]{:T(128)S(6)} %select_n.132), kind=kLoop, calls=%fused_computation.36 | loop fusion | bytes 28 | tf_op jit(solution)/shard_map/dynamic_slice | solution.py:64
  14.5 0.7 constant_dynamic-slice_fusion.4
  16.1 1.1 %copy.15 = bf16[256,384]{0,1:T(8,128)(2,1)S(1)} copy(bf16[256,384]{1,0:T(8,128)(2,1)} %param.6) | data formatting | bytes 393216 | tf_op args[0]
  18.7 24.0 %collective-permute-done.1 = bf16[2,256,384]{1,2,0:T(8,128)(2,1)} collective-permute-done((bf16[2,256,384]{1,2,0:T(8,128)(2,1)}, bf16[2,256,384]{1,2,0:T(8,128)(2,1)}, u32[]{:S(2)}, u32[]{:S(2)}) %collective-permute-start.1) | collective-permute-done | bytes 393248 | tf_op jit(solution)/shard_map/ppermute | solution.py:16
  42.7 1.3 %pad_maximum_fusion = bf16[2,1024,384]{1,2,0:T(8,128)(2,1)S(1)} fusion(bf16[2,256,384]{1,2,0:T(8,128)(2,1)S(1)} %collective-permute-done.2, bf16[2,256,384]{1,2,0:T(8,128)(2,1)} %collective-permute-done.1, bf16[2,256,384]{1,2,0:T(8,128)(2,1)} %collective-permute-done, bf16[1,256,384]{1,2,0:T(8,128)(2,1)S(1)} %bitcast.82, bf16[1,256,384]{1,2,0:T(8,128)(2,1)S(1)} %bitcast.80), kind=kLoop, calls=%fused_computation.7 | loop fusion | flops 7864320 | bytes 3145728 | tf_op jit(solution)/shard_map/concatenate | solution.py:30
  44.8 0.8 %fusion.1 = (f32[3,256]{1,0:T(4,128)S(1)}, bf16[3,256,1024]{1,2,0:T(8,128)(2,1)S(1)}) fusion(f32[3,1024,256]{2,1,0:T(8,128)S(1)} %get-tuple-element.13, f32[3,256]{1,0:T(4,128)S(1)} %get-tuple-element.12, pred[3,256,8]{1,2,0:T(8,128)(4,1)S(1)} %broadcast_bitcast_fusion), kind=kLoop, calls=%fused_computation.5 | loop fusion | flops 4717824 | bytes 4730880 | tf_op jit(solution)/shard_map/reduce_sum | solution.py:47
  45.7 2.8 %collective-permute-start.7 = (f32[3,256]{1,0:T(4,128)S(1)}, f32[3,256]{1,0:T(4,128)S(1)}, u32[]{:S(2)}, u32[]{:S(2)}) collective-permute-start(f32[3,256]{1,0:T(4,128)S(1)} %log_add_fusion), channel_id=1, source_target_pairs={{0,8},{4,12},{8,0},{12,4},{1,9},{5,13},{9,1},{13,5},{2,10},{6,14},... | collective-permute-start | bytes 9224 | tf_op jit(solution)/shard_map/ppermute | solution.py:16
  48.5 1.9 %collective-permute-start.6 = (f32[3,256]{1,0:T(4,128)S(1)}, f32[3,256]{1,0:T(4,128)S(1)}, u32[]{:S(2)}, u32[]{:S(2)}) collective-permute-start(f32[3,256]{1,0:T(4,128)S(1)} %log_add_fusion), channel_id=1, source_target_pairs={{0,4},{4,8},{8,12},{12,0},{1,5},{5,9},{9,13},{13,1},{2,6},{6,10},{... | collective-permute-start | bytes 9224 | tf_op jit(solution)/shard_map/ppermute | solution.py:16
  50.9 2.6 %fusion.14 = (bf16[256,3072]{1,0:T(8,128)(2,1)S(1)}, f32[256,3072]{1,0:T(8,128)}) fusion(bf16[256,384]{0,1:T(8,128)(2,1)S(1)} %bitcast.85, bf16[384,3072]{1,0:T(8,128)(2,1)S(1)} %copy-done), kind=kOutput, calls=%fused_computation.53 | convolution fusion | flops 604766208 | bytes 7274496 | tf_op jit(solution)/shard_map/dot_general | solution.py:72
  53.5 0.8 %dynamic-slice_bitcast_fusion.2 = (bf16[64,3072]{1,0:T(8,128)(2,1)}, bf16[64,3072]{1,0:T(8,128)(2,1)S(1)}, bf16[64,3072]{1,0:T(8,128)(2,1)S(1)}) fusion(bf16[4,64,3072]{2,1,0:T(8,128)(2,1)S(1)} %bitcast.77, s32[]{:T(128)S(6)} %select_n.127, s32[]{:T(128)S(6)} %select_n.131, s32[]{:T(128)S(6)} %select_n.129), kind=kLoop, calls=%fused_computation.18 | loop fusion | bytes 2359308 | tf_op jit(solution)/shard_map/squeeze | solution.py:81
  54.4 1.7 %collective-permute-start.5 = (bf16[64,3072]{1,0:T(8,128)(2,1)S(1)}, bf16[64,3072]{1,0:T(8,128)(2,1)}, u32[]{:S(2)}, u32[]{:S(2)}) collective-permute-start(bf16[64,3072]{1,0:T(8,128)(2,1)S(1)} %get-tuple-element.5), channel_id=1, source_target_pairs={{0,3},{1,0},{2,1},{3,2},{4,7},{5,4},{6,5},{7,6},{8,11},{9,8},{10,9... | collective-permute-start | bytes 1179656 | tf_op jit(solution)/shard_map/ppermute | solution.py:82
  56.1 1.5 %collective-permute-start.4 = (bf16[64,3072]{1,0:T(8,128)(2,1)S(1)}, bf16[64,3072]{1,0:T(8,128)(2,1)}, u32[]{:S(2)}, u32[]{:S(2)}) collective-permute-start(bf16[64,3072]{1,0:T(8,128)(2,1)S(1)} %get-tuple-element.6), channel_id=1, source_target_pairs={{0,2},{1,3},{2,0},{3,1},{4,6},{5,7},{6,4},{7,5},{8,10},{9,11},{10,... | collective-permute-start | bytes 1179656 | tf_op jit(solution)/shard_map/ppermute | solution.py:82
  57.6 1.3 %gather_fusion.1 = f32[4,3,256]{2,1,0:T(4,128)} fusion(f32[4,3,256]{2,1,0:T(4,128)S(1)} %pad_maximum_fusion.2, s32[1024]{0:T(1024)} %pad_clamp_fusion), kind=kCustom, calls=%fused_computation.1 | custom fusion | bytes 24592 | tf_op jit(solution)/shard_map/jit(_take)/gather | solution.py:60
  58.9 0.8 %broadcast_select_fusion = f32[4,3,256]{2,1,0:T(4,128)S(1)} fusion(f32[4,3,256]{2,1,0:T(4,128)} %gather_fusion.1, pred[4]{0:T(512)(128)(4,1)} %compare_and_fusion), kind=kLoop, calls=%fused_computation.23 | loop fusion | flops 3072 | bytes 24580 | tf_op jit(solution)/shard_map/jit(_take)/select_n | solution.py:60
  59.7 0.7 fusion.8
  60.4 4.0 %collective-permute-done.3 = bf16[64,3072]{1,0:T(8,128)(2,1)S(1)} collective-permute-done((bf16[64,3072]{1,0:T(8,128)(2,1)}, bf16[64,3072]{1,0:T(8,128)(2,1)S(1)}, u32[]{:S(2)}, u32[]{:S(2)}) %collective-permute-start.3) | collective-permute-done | bytes 393248 | tf_op jit(solution)/shard_map/ppermute | solution.py:82
  64.4 1.2 %collective-permute-done.5 = bf16[64,3072]{1,0:T(8,128)(2,1)} collective-permute-done((bf16[64,3072]{1,0:T(8,128)(2,1)S(1)}, bf16[64,3072]{1,0:T(8,128)(2,1)}, u32[]{:S(2)}, u32[]{:S(2)}) %collective-permute-start.5) | collective-permute-done | bytes 393248 | tf_op jit(solution)/shard_map/ppermute | solution.py:82
  65.6 8.9 %collective-permute-done.4 = bf16[64,3072]{1,0:T(8,128)(2,1)} collective-permute-done((bf16[64,3072]{1,0:T(8,128)(2,1)S(1)}, bf16[64,3072]{1,0:T(8,128)(2,1)}, u32[]{:S(2)}, u32[]{:S(2)}) %collective-permute-start.4) | collective-permute-done | bytes 393248 | tf_op jit(solution)/shard_map/ppermute | solution.py:82
  74.5 2.3 %fusion.7 = bf16[64,3072]{1,0:T(8,128)(2,1)} fusion(bf16[64,3072]{1,0:T(8,128)(2,1)} %collective-permute-done.5, bf16[64,3072]{1,0:T(8,128)(2,1)} %collective-permute-done.4, bf16[64,3072]{1,0:T(8,128)(2,1)S(1)} %collective-permute-done.3, f32[4,64,3072]{2,1,0:T(8,128)} %bitcast.76, s32[]{:T(128)S(6)} %select_n.125), kind=kLoop, calls=%fused_computation.14 | loop fusion | flops 1376256 | bytes 2359300 | tf_op jit(solution)/shard_map/convert_element_type | solution.py:83
  (31 shorter events, 3.9 us)
Async XLA Ops:
  0.6 50.3 %copy-start = (bf16[384,3072]{1,0:T(8,128)(2,1)S(1)}, bf16[384,3072]{1,0:T(8,128)(2,1)}, u32[]{:S(2)}) copy-start(bf16[384,3072]{1,0:T(8,128)(2,1)} %param.11) | copy-start | bytes 7077892
  3.7 14.9 %collective-permute-start.2 = (bf16[2,256,384]{1,2,0:T(8,128)(2,1)}, bf16[2,256,384]{1,2,0:T(8,128)(2,1)S(1)}, u32[]{:S(2)}, u32[]{:S(2)}) collective-permute-start(bf16[2,256,384]{1,2,0:T(8,128)(2,1)} %pad_maximum_fusion.1), channel_id=1, source_target_pairs={{0,12},{4,0},{8,4},{12,8},{1,13},{5,1},{9,5},{13,9},{2,14},{6,2},{... | collective-permute-start | bytes 1179656 | tf_op jit(solution)/shard_map/ppermute | solution.py:16
  8.8 33.9 %collective-permute-start.1 = (bf16[2,256,384]{1,2,0:T(8,128)(2,1)}, bf16[2,256,384]{1,2,0:T(8,128)(2,1)}, u32[]{:S(2)}, u32[]{:S(2)}) collective-permute-start(bf16[2,256,384]{1,2,0:T(8,128)(2,1)} %pad_maximum_fusion.1), channel_id=1, source_target_pairs={{0,8},{4,12},{8,0},{12,4},{1,9},{5,13},{9,1},{13,5},{2,10},{6,14},... | collective-permute-start | bytes 1179656 | tf_op jit(solution)/shard_map/ppermute | solution.py:16
  8.8 33.9 %collective-permute-start = (bf16[2,256,384]{1,2,0:T(8,128)(2,1)}, bf16[2,256,384]{1,2,0:T(8,128)(2,1)}, u32[]{:S(2)}, u32[]{:S(2)}) collective-permute-start(bf16[2,256,384]{1,2,0:T(8,128)(2,1)} %pad_maximum_fusion.1), channel_id=1, source_target_pairs={{0,4},{4,8},{8,12},{12,0},{1,5},{5,9},{9,13},{13,1},{2,6},{6,10},{... | collective-permute-start | bytes 1179656 | tf_op jit(solution)/shard_map/ppermute | solution.py:16
  45.6 10.5 %collective-permute-start.8 = (f32[3,256]{1,0:T(4,128)S(1)}, f32[3,256]{1,0:T(4,128)S(1)}, u32[]{:S(2)}, u32[]{:S(2)}) collective-permute-start(f32[3,256]{1,0:T(4,128)S(1)} %log_add_fusion), channel_id=1, source_target_pairs={{0,12},{4,0},{8,4},{12,8},{1,13},{5,1},{9,5},{13,9},{2,14},{6,2},{... | collective-permute-start | bytes 9224 | tf_op jit(solution)/shard_map/ppermute | solution.py:16
  45.7 11.9 %collective-permute-start.7 = (f32[3,256]{1,0:T(4,128)S(1)}, f32[3,256]{1,0:T(4,128)S(1)}, u32[]{:S(2)}, u32[]{:S(2)}) collective-permute-start(f32[3,256]{1,0:T(4,128)S(1)} %log_add_fusion), channel_id=1, source_target_pairs={{0,8},{4,12},{8,0},{12,4},{1,9},{5,13},{9,1},{13,5},{2,10},{6,14},... | collective-permute-start | bytes 9224 | tf_op jit(solution)/shard_map/ppermute | solution.py:16
  48.5 9.1 %collective-permute-start.6 = (f32[3,256]{1,0:T(4,128)S(1)}, f32[3,256]{1,0:T(4,128)S(1)}, u32[]{:S(2)}, u32[]{:S(2)}) collective-permute-start(f32[3,256]{1,0:T(4,128)S(1)} %log_add_fusion), channel_id=1, source_target_pairs={{0,4},{4,8},{8,12},{12,0},{1,5},{5,9},{9,13},{13,1},{2,6},{6,10},{... | collective-permute-start | bytes 9224 | tf_op jit(solution)/shard_map/ppermute | solution.py:16
  54.4 10.0 %collective-permute-start.3 = (bf16[64,3072]{1,0:T(8,128)(2,1)}, bf16[64,3072]{1,0:T(8,128)(2,1)S(1)}, u32[]{:S(2)}, u32[]{:S(2)}) collective-permute-start(bf16[64,3072]{1,0:T(8,128)(2,1)} %get-tuple-element.4), channel_id=1, source_target_pairs={{0,1},{1,2},{2,3},{3,0},{4,5},{5,6},{6,7},{7,4},{8,9},{9,10},{10,1... | collective-permute-start | bytes 1179656 | tf_op jit(solution)/shard_map/ppermute | solution.py:82
  54.4 11.2 %collective-permute-start.5 = (bf16[64,3072]{1,0:T(8,128)(2,1)S(1)}, bf16[64,3072]{1,0:T(8,128)(2,1)}, u32[]{:S(2)}, u32[]{:S(2)}) collective-permute-start(bf16[64,3072]{1,0:T(8,128)(2,1)S(1)} %get-tuple-element.5), channel_id=1, source_target_pairs={{0,3},{1,0},{2,1},{3,2},{4,7},{5,4},{6,5},{7,6},{8,11},{9,8},{10,9... | collective-permute-start | bytes 1179656 | tf_op jit(solution)/shard_map/ppermute | solution.py:82
  56.1 18.4 %collective-permute-start.4 = (bf16[64,3072]{1,0:T(8,128)(2,1)S(1)}, bf16[64,3072]{1,0:T(8,128)(2,1)}, u32[]{:S(2)}, u32[]{:S(2)}) collective-permute-start(bf16[64,3072]{1,0:T(8,128)(2,1)S(1)} %get-tuple-element.6), channel_id=1, source_target_pairs={{0,2},{1,3},{2,0},{3,1},{4,6},{5,7},{6,4},{7,5},{8,10},{9,11},{10,... | collective-permute-start | bytes 1179656 | tf_op jit(solution)/shard_map/ppermute | solution.py:82

commit v6 on v5

--- a/solution.py
+++ b/solution.py
@@ -69,17 +69,22 @@
     unit_norm = jnp.where(
         jnp.arange(slab_most * BLK, dtype=jnp.int32) < own_length * BLK, unit_norm, 0.0
     )
-    partial = jnp.dot(attn_local, out_weight, preferred_element_type=jnp.float32)
     rep_count = lax.axis_size("rep")
     peer_count = lax.axis_size("sub") * rep_count
     peer_index = lax.axis_index("sub") * rep_count + lax.axis_index("rep")
     chunk = tok_count // peer_count
-    chunks = partial.astype(jnp.bfloat16).reshape(peer_count, chunk, partial.shape[1])
-    summed = partial.reshape(peer_count, chunk, partial.shape[1])[peer_index]
+    received = []
     for shift in range(1, peer_count):
         pairs = [(source, (source + shift) % peer_count) for source in range(peer_count)]
-        sent = chunks[(peer_index + shift) % peer_count]
-        summed = summed + lax.ppermute(sent, ("sub", "rep"), pairs).astype(jnp.float32)
+        rows = lax.dynamic_slice_in_dim(
+            attn_local, ((peer_index + shift) % peer_count) * chunk, chunk, 0
+        )
+        sent = jnp.dot(rows, out_weight, preferred_element_type=jnp.float32)
+        received.append(lax.ppermute(sent.astype(jnp.bfloat16), ("sub", "rep"), pairs))
+    own_rows = lax.dynamic_slice_in_dim(attn_local, peer_index * chunk, chunk, 0)
+    summed = jnp.dot(own_rows, out_weight, preferred_element_type=jnp.float32)
+    for piece in received:
+        summed = summed + piece.astype(jnp.float32)
     return (summed.astype(jnp.bfloat16), unit_norm.reshape(1, 1, slab_most * BLK))
 
 

time: 77.2 us -> 75.3 us (0.975)
  other arithmetic: 8.07 us -> 3.91 us
  matrix products: 3.7 us -> 7.59 us
  local copies, waits for them, and re-layouts: 8.65 us -> 7.15 us
  starting transfers between devices: 14.2 us -> 12.7 us
  waiting for transfers between devices: 38.3 us -> 39.5 us
    dot_general x1 -> x4, matrix products: 2.64 us -> 6.56 us  [the longest x3 4.12 us: local(): sent = jnp.dot(rows, out_weight, preferred_element_type=jnp.float32)]
    convert_element_type x1 -> x0, other arithmetic: 2.29 us -> none  [local(): summed.astype(jnp.bfloat16)]
    ppermute x3, starting transfers between devices: 3.24 us -> 1.74 us  [local(): lax.ppermute(sent.astype(jnp.bfloat16), ('sub', 'rep'), pairs)]
    ppermute x6, waiting for transfers between devices: 24.2 us -> 25.1 us  [around(): pieces.append(lax.ppermute(piece, 'seq', pairs))]
    squeeze x1 -> x0, local copies, waits for them, and re-layouts: 0.84 us -> none  [local(): sent = chunks[(peer_index + shift) % peer_count]]
  transfers between devices with their start and end apart: 9 -> 9, of which waited for: 5 -> 5; matrix products, arithmetic and copies ran while one was open for 16% -> 14% of each run, Pallas kernels for 0% -> 0%
where the time goes in v6:
time: 75.3 us; the launch traced here: 74.9 us
  waiting for transfers between devices  39.5 us (52%)
  starting transfers between devices  12.7 us (17%)
  matrix products  7.59 us (10%)
  local copies, waits for them, and re-layouts  7.15 us (9%)
  between operations  4.07 us (5%)
  other arithmetic  3.91 us (5%)
    ppermute x6, waiting for transfers between devices, around(): pieces.append(lax.ppermute(piece, 'seq', pairs))  25.1 us
    ppermute x3, waiting for transfers between devices, local(): lax.ppermute(sent.astype(jnp.bfloat16), ('sub', 'rep'), pairs)  14.4 us
    ppermute x6, starting transfers between devices, around(): pieces.append(lax.ppermute(piece, 'seq', pairs))  11 us
    dot_general x3, matrix products, local(): sent = jnp.dot(rows, out_weight, preferred_element_type=jnp.float32)  4.12 us
    unnamed x6, local copies, waits for them, and re-layouts  3.44 us
    dot_general x1, matrix products, local(): summed = jnp.dot(own_rows, out_weight, preferred_element_type=jnp.float32)  2.44 us
    ppermute x3, starting transfers between devices, local(): lax.ppermute(sent.astype(jnp.bfloat16), ('sub', 'rep'), pairs)  1.74 us
  transfers between devices with their start and end apart: 9, of which 5 were waited for; matrix products, arithmetic and copies ran while one was open for 14% of the time, Pallas kernels for 0%

profile of v6, /device:TPU:0, one launch (start us, length us, event | category | flops | bytes accessed | tf_op | source)
XLA Modules:
  0.0 74.9 jit_solution(10024582994998177914)
XLA Ops:
  0.6 1.2 %copy.14 = bf16[256,384]{0,1:T(8,128)(2,1)S(1)} copy(bf16[256,384]{1,0:T(8,128)(2,1)} %param.8) | data formatting | bytes 393216 | tf_op args[2]
  1.9 1.1 %copy.13 = bf16[256,384]{0,1:T(8,128)(2,1)S(1)} copy(bf16[256,384]{1,0:T(8,128)(2,1)} %param.7) | data formatting | bytes 393216 | tf_op args[1]
  2.9 0.8 %pad_maximum_fusion.1 = bf16[2,256,384]{1,2,0:T(8,128)(2,1)} fusion(bf16[1,256,384]{1,2,0:T(8,128)(2,1)S(1)} %bitcast.63, bf16[1,256,384]{1,2,0:T(8,128)(2,1)S(1)} %bitcast.65), kind=kLoop, calls=%fused_computation.15 | loop fusion | flops 196608 | bytes 786432 | tf_op jit(solution)/shard_map/stack | solution.py:29
  3.7 5.1 %collective-permute-start.2 = (bf16[2,256,384]{1,2,0:T(8,128)(2,1)}, bf16[2,256,384]{1,2,0:T(8,128)(2,1)S(1)}, u32[]{:S(2)}, u32[]{:S(2)}) collective-permute-start(bf16[2,256,384]{1,2,0:T(8,128)(2,1)} %pad_maximum_fusion.1), channel_id=1, source_target_pairs={{0,12},{4,0},{8,4},{12,8},{1,13},{5,1},{9,5},{13,9},{2,14},{6,2},{... | collective-permute-start | bytes 1179656 | tf_op jit(solution)/shard_map/ppermute | solution.py:16
  8.8 1.0 %collective-permute-start = (bf16[2,256,384]{1,2,0:T(8,128)(2,1)}, bf16[2,256,384]{1,2,0:T(8,128)(2,1)}, u32[]{:S(2)}, u32[]{:S(2)}) collective-permute-start(bf16[2,256,384]{1,2,0:T(8,128)(2,1)} %pad_maximum_fusion.1), channel_id=1, source_target_pairs={{0,4},{4,8},{8,12},{12,0},{1,5},{5,9},{9,13},{13,1},{2,6},{6,10},{... | collective-permute-start | bytes 1179656 | tf_op jit(solution)/shard_map/ppermute | solution.py:16
  10.1 1.3 %constant_dynamic-slice_fusion.3 = (s32[1,1,1]{1,0,2:T(1,128)}, s32[1,1,1]{1,0,2:T(1,128)}, s32[1,1,1]{1,0,2:T(1,128)}) fusion(s32[1,4,3]{1,0,2:T(1,128)} %param.10, s32[]{:T(128)S(6)} %select_n.132), kind=kLoop, calls=%fused_computation.38 | loop fusion | bytes 28 | tf_op jit(solution)/shard_map/dynamic_slice | solution.py:64
  12.8 0.7 constant_dynamic-slice_fusion.4
  14.4 1.1 %copy.15 = bf16[256,384]{0,1:T(8,128)(2,1)S(1)} copy(bf16[256,384]{1,0:T(8,128)(2,1)} %param.6) | data formatting | bytes 393216 | tf_op args[0]
  17.5 1.1 %collective-permute-done.2 = bf16[2,256,384]{1,2,0:T(8,128)(2,1)S(1)} collective-permute-done((bf16[2,256,384]{1,2,0:T(8,128)(2,1)}, bf16[2,256,384]{1,2,0:T(8,128)(2,1)S(1)}, u32[]{:S(2)}, u32[]{:S(2)}) %collective-permute-start.2) | collective-permute-done | bytes 393248 | tf_op jit(solution)/shard_map/ppermute | solution.py:16
  18.7 24.0 %collective-permute-done.1 = bf16[2,256,384]{1,2,0:T(8,128)(2,1)} collective-permute-done((bf16[2,256,384]{1,2,0:T(8,128)(2,1)}, bf16[2,256,384]{1,2,0:T(8,128)(2,1)}, u32[]{:S(2)}, u32[]{:S(2)}) %collective-permute-start.1) | collective-permute-done | bytes 393248 | tf_op jit(solution)/shard_map/ppermute | solution.py:16
  42.7 1.3 %pad_maximum_fusion = bf16[2,1024,384]{1,2,0:T(8,128)(2,1)S(1)} fusion(bf16[2,256,384]{1,2,0:T(8,128)(2,1)S(1)} %collective-permute-done.2, bf16[2,256,384]{1,2,0:T(8,128)(2,1)} %collective-permute-done.1, bf16[2,256,384]{1,2,0:T(8,128)(2,1)} %collective-permute-done, bf16[1,256,384]{1,2,0:T(8,128)(2,1)S(1)} %bitcast.64, bf16[1,256,384]{1,2,0:T(8,128)(2,1)S(1)} %bitcast.66), kind=kLoop, calls=%fused_computation.10 | loop fusion | flops 7864320 | bytes 3145728 | tf_op jit(solution)/shard_map/concatenate | solution.py:30
  44.1 0.7 fusion
  44.8 0.8 %fusion.1 = (f32[3,256]{1,0:T(4,128)S(1)}, bf16[3,256,1024]{1,2,0:T(8,128)(2,1)S(1)}) fusion(f32[3,1024,256]{2,1,0:T(8,128)S(1)} %get-tuple-element.10, f32[3,256]{1,0:T(4,128)S(1)} %get-tuple-element.9, pred[3,256,8]{1,2,0:T(8,128)(4,1)S(1)} %broadcast_bitcast_fusion), kind=kLoop, calls=%fused_computation.8 | loop fusion | flops 4717824 | bytes 4730880 | tf_op jit(solution)/shard_map/reduce_sum | solution.py:47
  45.7 2.9 %collective-permute-start.7 = (f32[3,256]{1,0:T(4,128)S(1)}, f32[3,256]{1,0:T(4,128)S(1)}, u32[]{:S(2)}, u32[]{:S(2)}) collective-permute-start(f32[3,256]{1,0:T(4,128)S(1)} %log_add_fusion), channel_id=1, source_target_pairs={{0,8},{4,12},{8,0},{12,4},{1,9},{5,13},{9,1},{13,5},{2,10},{6,14},... | collective-permute-start | bytes 9224 | tf_op jit(solution)/shard_map/ppermute | solution.py:16
  48.5 1.9 %collective-permute-start.6 = (f32[3,256]{1,0:T(4,128)S(1)}, f32[3,256]{1,0:T(4,128)S(1)}, u32[]{:S(2)}, u32[]{:S(2)}) collective-permute-start(f32[3,256]{1,0:T(4,128)S(1)} %log_add_fusion), channel_id=1, source_target_pairs={{0,4},{4,8},{8,12},{12,0},{1,5},{5,9},{9,13},{13,1},{2,6},{6,10},{... | collective-permute-start | bytes 9224 | tf_op jit(solution)/shard_map/ppermute | solution.py:16
  50.9 1.4 %convolution_convert_fusion = bf16[64,3072]{1,0:T(8,128)(2,1)} fusion(bf16[384,3072]{1,0:T(8,128)(2,1)S(1)} %copy-done, bf16[256,384]{0,1:T(8,128)(2,1)S(1)} %bitcast.67, s32[]{:T(128)S(6)} %select_n.131), kind=kOutput, calls=%fused_computation.4 | convolution fusion | flops 151191552 | bytes 2850820 | tf_op jit(solution)/shard_map/dot_general | solution.py:82
  52.3 1.4 %convolution_convert_fusion.1 = bf16[64,3072]{1,0:T(8,128)(2,1)} fusion(bf16[384,3072]{1,0:T(8,128)(2,1)S(1)} %copy-done, bf16[256,384]{0,1:T(8,128)(2,1)S(1)} %bitcast.68, s32[]{:T(128)S(6)} %select_n.129), kind=kOutput, calls=%fused_computation.5 | convolution fusion | flops 151191552 | bytes 2850820 | tf_op jit(solution)/shard_map/dot_general | solution.py:82
  53.6 1.5 %collective-permute-start.4 = (bf16[64,3072]{1,0:T(8,128)(2,1)}, bf16[64,3072]{1,0:T(8,128)(2,1)S(1)}, u32[]{:S(2)}, u32[]{:S(2)}) collective-permute-start(bf16[64,3072]{1,0:T(8,128)(2,1)} %convolution_convert_fusion.1), channel_id=1, source_target_pairs={{0,2},{1,3},{2,0},{3,1},{4,6},{5,7},{6,4},{7,5},{8,10},{9,11},{10,... | collective-permute-start | bytes 1179656 | tf_op jit(solution)/shard_map/ppermute | solution.py:83
  55.1 1.4 %convolution_convert_fusion.2 = bf16[64,3072]{1,0:T(8,128)(2,1)} fusion(bf16[384,3072]{1,0:T(8,128)(2,1)S(1)} %copy-done, bf16[256,384]{0,1:T(8,128)(2,1)S(1)} %bitcast.69, s32[]{:T(128)S(6)} %select_n.127), kind=kOutput, calls=%fused_computation.6 | convolution fusion | flops 151191552 | bytes 2850820 | tf_op jit(solution)/shard_map/dot_general | solution.py:82
  57.4 0.7 fusion.12
  58.1 1.6 %collective-permute-done.5 = bf16[64,3072]{1,0:T(8,128)(2,1)S(1)} collective-permute-done((bf16[64,3072]{1,0:T(8,128)(2,1)}, bf16[64,3072]{1,0:T(8,128)(2,1)S(1)}, u32[]{:S(2)}, u32[]{:S(2)}) %collective-permute-start.5) | collective-permute-done | bytes 393248 | tf_op jit(solution)/shard_map/ppermute | solution.py:83
  59.7 11.3 %collective-permute-done.4 = bf16[64,3072]{1,0:T(8,128)(2,1)S(1)} collective-permute-done((bf16[64,3072]{1,0:T(8,128)(2,1)}, bf16[64,3072]{1,0:T(8,128)(2,1)S(1)}, u32[]{:S(2)}, u32[]{:S(2)}) %collective-permute-start.4) | collective-permute-done | bytes 393248 | tf_op jit(solution)/shard_map/ppermute | solution.py:83
  70.9 1.5 %collective-permute-done.3 = bf16[64,3072]{1,0:T(8,128)(2,1)} collective-permute-done((bf16[64,3072]{1,0:T(8,128)(2,1)}, bf16[64,3072]{1,0:T(8,128)(2,1)}, u32[]{:S(2)}, u32[]{:S(2)}) %collective-permute-start.3) | collective-permute-done | bytes 393248 | tf_op jit(solution)/shard_map/ppermute | solution.py:83
  72.5 2.4 %add_convert_fusion = bf16[64,3072]{1,0:T(8,128)(2,1)} fusion(bf16[64,3072]{1,0:T(8,128)(2,1)S(1)} %collective-permute-done.5, bf16[64,3072]{1,0:T(8,128)(2,1)S(1)} %collective-permute-done.4, bf16[64,3072]{1,0:T(8,128)(2,1)} %collective-permute-done.3, bf16[384,3072]{1,0:T(8,128)(2,1)S(1)} %copy-done, bf16[256,384]{0,1:T(8,128)(2,1)S(1)} %bitcast.70, ...), kind=kOutput, calls=%fused_computation.14 | convolution fusion | flops 152371200 | bytes 4030468 | tf_op jit(solution)/shard_map/dot_general | solution.py:85
  (32 shorter events, 2.7 us)
Async XLA Ops:
  0.6 50.2 %copy-start = (bf16[384,3072]{1,0:T(8,128)(2,1)S(1)}, bf16[384,3072]{1,0:T(8,128)(2,1)}, u32[]{:S(2)}) copy-start(bf16[384,3072]{1,0:T(8,128)(2,1)} %param.11) | copy-start | bytes 7077892
  3.7 14.9 %collective-permute-start.2 = (bf16[2,256,384]{1,2,0:T(8,128)(2,1)}, bf16[2,256,384]{1,2,0:T(8,128)(2,1)S(1)}, u32[]{:S(2)}, u32[]{:S(2)}) collective-permute-start(bf16[2,256,384]{1,2,0:T(8,128)(2,1)} %pad_maximum_fusion.1), channel_id=1, source_target_pairs={{0,12},{4,0},{8,4},{12,8},{1,13},{5,1},{9,5},{13,9},{2,14},{6,2},{... | collective-permute-start | bytes 1179656 | tf_op jit(solution)/shard_map/ppermute | solution.py:16
  8.8 33.9 %collective-permute-start.1 = (bf16[2,256,384]{1,2,0:T(8,128)(2,1)}, bf16[2,256,384]{1,2,0:T(8,128)(2,1)}, u32[]{:S(2)}, u32[]{:S(2)}) collective-permute-start(bf16[2,256,384]{1,2,0:T(8,128)(2,1)} %pad_maximum_fusion.1), channel_id=1, source_target_pairs={{0,8},{4,12},{8,0},{12,4},{1,9},{5,13},{9,1},{13,5},{2,10},{6,14},... | collective-permute-start | bytes 1179656 | tf_op jit(solution)/shard_map/ppermute | solution.py:16
  8.8 33.9 %collective-permute-start = (bf16[2,256,384]{1,2,0:T(8,128)(2,1)}, bf16[2,256,384]{1,2,0:T(8,128)(2,1)}, u32[]{:S(2)}, u32[]{:S(2)}) collective-permute-start(bf16[2,256,384]{1,2,0:T(8,128)(2,1)} %pad_maximum_fusion.1), channel_id=1, source_target_pairs={{0,4},{4,8},{8,12},{12,0},{1,5},{5,9},{9,13},{13,1},{2,6},{6,10},{... | collective-permute-start | bytes 1179656 | tf_op jit(solution)/shard_map/ppermute | solution.py:16
  45.6 10.9 %collective-permute-start.8 = (f32[3,256]{1,0:T(4,128)S(1)}, f32[3,256]{1,0:T(4,128)S(1)}, u32[]{:S(2)}, u32[]{:S(2)}) collective-permute-start(f32[3,256]{1,0:T(4,128)S(1)} %log_add_fusion), channel_id=1, source_target_pairs={{0,12},{4,0},{8,4},{12,8},{1,13},{5,1},{9,5},{13,9},{2,14},{6,2},{... | collective-permute-start | bytes 9224 | tf_op jit(solution)/shard_map/ppermute | solution.py:16
  45.7 11.1 %collective-permute-start.7 = (f32[3,256]{1,0:T(4,128)S(1)}, f32[3,256]{1,0:T(4,128)S(1)}, u32[]{:S(2)}, u32[]{:S(2)}) collective-permute-start(f32[3,256]{1,0:T(4,128)S(1)} %log_add_fusion), channel_id=1, source_target_pairs={{0,8},{4,12},{8,0},{12,4},{1,9},{5,13},{9,1},{13,5},{2,10},{6,14},... | collective-permute-start | bytes 9224 | tf_op jit(solution)/shard_map/ppermute | solution.py:16
  48.5 8.2 %collective-permute-start.6 = (f32[3,256]{1,0:T(4,128)S(1)}, f32[3,256]{1,0:T(4,128)S(1)}, u32[]{:S(2)}, u32[]{:S(2)}) collective-permute-start(f32[3,256]{1,0:T(4,128)S(1)} %log_add_fusion), channel_id=1, source_target_pairs={{0,4},{4,8},{8,12},{12,0},{1,5},{5,9},{9,13},{13,1},{2,6},{6,10},{... | collective-permute-start | bytes 9224 | tf_op jit(solution)/shard_map/ppermute | solution.py:16
  52.3 7.4 %collective-permute-start.5 = (bf16[64,3072]{1,0:T(8,128)(2,1)}, bf16[64,3072]{1,0:T(8,128)(2,1)S(1)}, u32[]{:S(2)}, u32[]{:S(2)}) collective-permute-start(bf16[64,3072]{1,0:T(8,128)(2,1)} %convolution_convert_fusion), channel_id=1, source_target_pairs={{0,3},{1,0},{2,1},{3,2},{4,7},{5,4},{6,5},{7,6},{8,11},{9,8},{10,9... | collective-permute-start | bytes 1179656 | tf_op jit(solution)/shard_map/ppermute | solution.py:83
  53.6 17.3 %collective-permute-start.4 = (bf16[64,3072]{1,0:T(8,128)(2,1)}, bf16[64,3072]{1,0:T(8,128)(2,1)S(1)}, u32[]{:S(2)}, u32[]{:S(2)}) collective-permute-start(bf16[64,3072]{1,0:T(8,128)(2,1)} %convolution_convert_fusion.1), channel_id=1, source_target_pairs={{0,2},{1,3},{2,0},{3,1},{4,6},{5,7},{6,4},{7,5},{8,10},{9,11},{10,... | collective-permute-start | bytes 1179656 | tf_op jit(solution)/shard_map/ppermute | solution.py:83
  56.5 16.0 %collective-permute-start.3 = (bf16[64,3072]{1,0:T(8,128)(2,1)}, bf16[64,3072]{1,0:T(8,128)(2,1)}, u32[]{:S(2)}, u32[]{:S(2)}) collective-permute-start(bf16[64,3072]{1,0:T(8,128)(2,1)} %convolution_convert_fusion.2), channel_id=1, source_target_pairs={{0,1},{1,2},{2,3},{3,0},{4,5},{5,6},{6,7},{7,4},{8,9},{9,10},{10,1... | collective-permute-start | bytes 1179656 | tf_op jit(solution)/shard_map/ppermute | solution.py:83
